TPU v7x, 512 devices: a whole 4x8x8 slice. The times are simulated.
512 devices in a mesh: span: 8 (over z), chord: 8 (over x, y_lo), normal: 8 (over y_hi, core).
Axes of the slice: x: 4, y: 8 (y_hi: 4, y_lo: 2; y = y_hi * 2 + y_lo), z: 8, core: 2. Of those that a mesh axis runs over, the one named last changes fastest.
Arguments:
- state: float32 [5, 128, 64, 1024], P(None, 'chord', 'normal', 'span'), may hold values from -0.5 to 5
- metrics: float32 [9, 128, 64, 1024], P(None, 'chord', 'normal', 'span'), may hold values from -1 to 1
- face_codes: int32 [8, 8, 8, 6], P('chord', 'normal', 'span'), may hold values from 0 to 4, as said below
- inverse_i: float32 [8, 8, 8, 16, 16], P('chord', 'normal', 'span'), may hold values from -1 to 1
- inverse_j: float32 [8, 8, 8, 8, 8], P('chord', 'normal', 'span'), may hold values from -1 to 1
- inverse_k: float32 [8, 8, 8, 128, 128], P('chord', 'normal', 'span'), may hold values from -1 to 1
Outputs:
- increment: float32 [5, 128, 64, 1024], P(None, 'chord', 'normal', 'span')
Inputs may be any that keep to these rules, and one draw needn't show every extreme that they name: `face_codes`: for each block, the codes of its lower and upper chordwise faces, lower and upper wall-normal faces, lower and upper spanwise faces, in that order: 0 for a boundary face, else 1 plus two orientation bits; a face and the facing face of its neighbour block along that direction carry the same code.
All inputs are finite; a program needn't handle non-finite values.
Results may differ from a plain program's by a relative error of at most 0.0001.
Values sent between devices are 32-bit elements; how exact they have to be, the bound alone decides.
A program may use at most 64 MiB of HBM per device.

v0:
```python
import jax
import jax.numpy as jnp
from jax import lax
from jax.sharding import PartitionSpec as P

ITERS = 2


gas_factor = 0.4
damping = 0.1
pseudo_step = 0.03


def padded_2(array, sides, width):
    for axis, dim in sides:
        devices, length = (lax.axis_size(axis), array.shape[dim])
        up = [(i, (i + 1) % devices) for i in range(devices)]
        down = [(j, i) for i, j in up]
        last = lax.slice_in_dim(array, length - width, length, axis=dim)
        leading = lax.slice_in_dim(array, 0, width, axis=dim)
        before = lax.ppermute(last, axis, up)
        after = lax.ppermute(leading, axis, down)
        array = jnp.concatenate([before, array, after], axis=dim)
    return array


def in_face(direction):
    return [1 + other for other in range(3) if other != direction]


def orient(slab, code, axes_in):
    for power, axis_in in enumerate(axes_in):
        flag = jnp.logical_and(code > 0, (code - 1) // 2**power % 2 == 1)
        slab = jnp.where(flag, jnp.flip(slab, axis=axis_in), slab)
    return slab


def edges(block, direction, width):
    axis_cell = 1 + direction
    length = block.shape[axis_cell]
    return (
        lax.slice_in_dim(block, 0, width, axis=axis_cell),
        lax.slice_in_dim(block, length - width, length, axis=axis_cell),
    )


def assemble(block, direction, width, from_below, from_above, codes):
    lower, upper = edges(block, direction, width)
    axis_cell = 1 + direction
    ghost_low = jnp.where(codes[2 * direction] > 0, from_below, jnp.flip(lower, axis=axis_cell))
    ghost_high = jnp.where(
        codes[2 * direction + 1] > 0, from_above, jnp.flip(upper, axis=axis_cell)
    )
    return jnp.concatenate([ghost_low, block, ghost_high], axis=axis_cell)


def from_halo(padded, block, direction, width, codes, trim):
    axes_in = in_face(direction)
    if trim:
        for other in axes_in:
            padded = lax.slice_in_dim(padded, width, width + block.shape[other], axis=other)
    axis_cell = 1 + direction
    length = block.shape[axis_cell]
    below = lax.slice_in_dim(padded, 0, width, axis=axis_cell)
    above = lax.slice_in_dim(padded, length + width, length + 2 * width, axis=axis_cell)
    return assemble(
        block,
        direction,
        width,
        orient(below, codes[2 * direction], axes_in),
        orient(above, codes[2 * direction + 1], axes_in),
        codes,
    )


def flux_of(fields, triple):
    density = fields[0]
    mom_x = fields[1]
    mom_y = fields[2]
    mom_z = fields[3]
    energy = fields[4]
    kinetic = 0.5 * (mom_x * mom_x + mom_y * mom_y + mom_z * mom_z) / density
    pressure = gas_factor * (energy - kinetic)
    speed = (triple[0] * mom_x + triple[1] * mom_y + triple[2] * mom_z) / density
    return jnp.stack(
        [
            density * speed,
            mom_x * speed + triple[0] * pressure,
            mom_y * speed + triple[1] * pressure,
            mom_z * speed + triple[2] * pressure,
            (energy + pressure) * speed,
        ]
    )


def residual(state, padded_states, padded_metrics):
    total = jnp.zeros(state.shape, jnp.float32)
    for direction in range(3):
        axis_cell = 1 + direction
        length = state.shape[axis_cell]
        fields = padded_states[direction]
        inner = lax.slice_in_dim(fields, 1, length + 3, axis=axis_cell)
        fluxes = flux_of(inner, padded_metrics[direction])
        central = 0.5 * (
            lax.slice_in_dim(fluxes, 2, length + 2, axis=axis_cell)
            - lax.slice_in_dim(fluxes, 0, length, axis=axis_cell)
        )
        parts = [
            lax.slice_in_dim(fields, offset, offset + length, axis=axis_cell) for offset in range(5)
        ]
        fourth = parts[0] - 4.0 * parts[1] + 6.0 * parts[2] - 4.0 * parts[3] + parts[4]
        total = total - central - damping * fourth
    return total


def line_solve(values, inverse_i, inverse_j, inverse_k):
    highest = lax.Precision.HIGHEST
    values = jnp.einsum("fijk,lk->fijl", values, inverse_k[0, 0, 0], precision=highest)
    values = jnp.einsum("fijk,lj->filk", values, inverse_j[0, 0, 0], precision=highest)
    return jnp.einsum("fijk,li->fljk", values, inverse_i[0, 0, 0], precision=highest)


def local(state, metrics, face_codes, inverse_i, inverse_j, inverse_k):
    codes = face_codes[0, 0, 0]
    xi_padded = padded_2(metrics[0:3], (("chord", 1),), 1)
    eta_padded = padded_2(metrics[3:6], (("normal", 2),), 1)
    zeta_padded = padded_2(metrics[6:9], (("span", 3),), 1)
    padded_metrics = [
        from_halo(xi_padded, metrics[0:3], 0, 1, codes, False),
        from_halo(eta_padded, metrics[3:6], 1, 1, codes, False),
        from_halo(zeta_padded, metrics[6:9], 2, 1, codes, False),
    ]
    total = jnp.zeros(state.shape, jnp.float32)
    current = state
    for sweep in range(ITERS):
        padded = padded_2(current, (("span", 3), ("chord", 1), ("normal", 2)), 2)
        padded_states = [
            from_halo(padded, current, direction, 2, codes, True) for direction in range(3)
        ]
        change = line_solve(
            residual(current, padded_states, padded_metrics), inverse_i, inverse_j, inverse_k
        )
        total = total + change
        current = current + pseudo_step * change
    return total


def solution(mesh):
    placed = (
        P(None, "chord", "normal", "span"),
        P(None, "chord", "normal", "span"),
        P("chord", "normal", "span", None),
        P("chord", "normal", "span", None, None),
        P("chord", "normal", "span", None, None),
        P("chord", "normal", "span", None, None),
    )
    return jax.shard_map(
        local,
        mesh=mesh,
        in_specs=placed,
        out_specs=P(None, "chord", "normal", "span"),
        check_vma=False,
    )
```

profile of v0, /device:TPU:1, one launch (start us, length us, event | category | flops | bytes accessed | tf_op | source)
XLA Modules:
  0.0 143.4 jit_solution(17305311515193018239)
XLA Ops:
  0.0 1.1 copy.7
  1.2 11.5 %collective-permute-start.1 = (f32[5,16,8,2]{3,1,2,0:T(8,128)S(1)}, f32[5,16,8,2]{3,1,2,0:T(8,128)S(1)}, u32[]{:S(2)}, u32[]{:S(2)}) collective-permute-start(f32[5,16,8,2]{3,1,2,0:T(8,128)S(1)} %get-tuple-element.71), channel_id=1, source_target_pairs={{64,0},{128,64},{192,128},{256,192},{320,256},{384,320},{448,384},... | collective-permute-start | bytes 15368 | tf_op jit(solution)/shard_map/ppermute | solution.py:22
  12.7 1.9 %collective-permute-start = (f32[5,16,8,2]{3,1,2,0:T(8,128)S(1)}, f32[5,16,8,2]{3,1,2,0:T(8,128)S(1)}, u32[]{:S(2)}, u32[]{:S(2)}) collective-permute-start(f32[5,16,8,2]{3,1,2,0:T(8,128)S(1)} %get-tuple-element.70), channel_id=1, source_target_pairs={{0,64},{64,128},{128,192},{192,256},{256,320},{320,384},{384,448},... | collective-permute-start | bytes 15368 | tf_op jit(solution)/shard_map/ppermute | solution.py:21
  14.7 0.7 fusion.105
  15.4 0.7 copy.48
  16.1 1.9 %collective-permute-start.10 = (f32[3,16,8,1]{3,1,2,0:T(8,128)}, f32[3,16,8,1]{3,1,2,0:T(8,128)}, u32[]{:S(2)}, u32[]{:S(2)}) collective-permute-start(f32[3,16,8,1]{3,1,2,0:T(8,128)} %copy.48), channel_id=1, source_target_pairs={{0,64},{64,128},{128,192},{192,256},{256,320},{320,384},{384,448},... | collective-permute-start | bytes 4616 | tf_op jit(solution)/shard_map/ppermute | solution.py:21
  18.0 0.6 fusion.104
  18.7 2.9 %collective-permute-start.9 = (f32[3,16,1,128]{3,1,2,0:T(8,128)S(1)}, f32[3,16,1,128]{3,1,2,0:T(8,128)S(1)}, u32[]{:S(2)}, u32[]{:S(2)}) collective-permute-start(f32[3,16,1,128]{3,1,2,0:T(8,128)S(1)} %bitcast.59), channel_id=1, source_target_pairs={{1,0},{2,1},{3,2},{4,3},{5,4},{6,5},{7,6},{0,7},{9,8},{10,9},{11,1... | collective-permute-start | bytes 73736 | tf_op jit(solution)/shard_map/ppermute | solution.py:22
  21.5 4.1 %collective-permute-start.8 = (f32[3,16,1,128]{3,1,2,0:T(8,128)}, f32[3,16,1,128]{3,1,2,0:T(8,128)S(1)}, u32[]{:S(2)}, u32[]{:S(2)}) collective-permute-start(f32[3,16,1,128]{3,1,2,0:T(8,128)} %bitcast.33), channel_id=1, source_target_pairs={{0,1},{1,2},{2,3},{3,4},{4,5},{5,6},{6,7},{7,0},{8,9},{9,10},{10,1... | collective-permute-start | bytes 73736 | tf_op jit(solution)/shard_map/ppermute | solution.py:21
  25.7 0.7 fusion.110
  26.5 0.5 copy-done.21
  27.0 0.7 fusion.112
  35.7 0.8 fusion.102
  36.5 0.6 fusion.103
  37.1 0.9 rev.185
  38.0 1.0 broadcast_select_fusion.5
  39.0 0.8 fusion.90
  39.8 5.0 %collective-permute-start.11 = (f32[3,16,8,1]{3,1,2,0:T(8,128)}, f32[3,16,8,1]{3,1,2,0:T(8,128)S(1)}, u32[]{:S(2)}, u32[]{:S(2)}) collective-permute-start(f32[3,16,8,1]{3,1,2,0:T(8,128)} %get-tuple-element.73), channel_id=1, source_target_pairs={{64,0},{128,64},{192,128},{256,192},{320,256},{384,320},{448,384},... | collective-permute-start | bytes 4616 | tf_op jit(solution)/shard_map/ppermute | solution.py:22
  44.9 0.7 rev.161
  45.7 0.7 copy.50
  46.7 0.7 copy.47
  47.4 0.7 copy.44
  48.5 6.1 %collective-permute-start.5 = (f32[3,1,8,128]{3,1,2,0:T(1,128)}, f32[3,1,8,128]{3,1,2,0:T(1,128)S(1)}, u32[]{:S(2)}, u32[]{:S(2)}) collective-permute-start(f32[3,1,8,128]{3,1,2,0:T(1,128)} %bitcast.32), channel_id=1, source_target_pairs={{8,0},{16,8},{24,16},{32,24},{40,32},{48,40},{56,48},{0,56},{9,1},... | collective-permute-start | bytes 36872 | tf_op jit(solution)/shard_map/ppermute | solution.py:22
  54.8 0.8 copy-done.13
  55.9 1.9 %collective-permute-start.4 = (f32[3,1,8,128]{3,1,2,0:T(1,128)}, f32[3,1,8,128]{3,1,2,0:T(1,128)S(1)}, u32[]{:S(2)}, u32[]{:S(2)}) collective-permute-start(f32[3,1,8,128]{3,1,2,0:T(1,128)} %bitcast.31), channel_id=1, source_target_pairs={{0,8},{8,16},{16,24},{24,32},{32,40},{40,48},{48,56},{56,0},{1,9},... | collective-permute-start | bytes 36872 | tf_op jit(solution)/shard_map/ppermute | solution.py:21
  58.7 5.5 %collective-permute-start.3 = (f32[5,2,8,132]{3,1,2,0:T(2,128)S(1)}, f32[5,2,8,132]{3,1,2,0:T(2,128)S(1)}, u32[]{:S(2)}, u32[]{:S(2)}) collective-permute-start(f32[5,2,8,132]{3,1,2,0:T(2,128)S(1)} %get-tuple-element.46), channel_id=1, source_target_pairs={{8,0},{16,8},{24,16},{32,24},{40,32},{48,40},{56,48},{0,56},{9,1},... | collective-permute-start | bytes 126728 | tf_op jit(solution)/shard_map/ppermute | solution.py:22
  65.0 0.9 copy-done.4
  65.8 2.0 %collective-permute-start.2 = (f32[5,2,8,132]{3,1,2,0:T(2,128)S(1)}, f32[5,2,8,132]{3,1,2,0:T(2,128)S(1)}, u32[]{:S(2)}, u32[]{:S(2)}) collective-permute-start(f32[5,2,8,132]{3,1,2,0:T(2,128)S(1)} %get-tuple-element.45), channel_id=1, source_target_pairs={{0,8},{8,16},{16,24},{24,32},{32,40},{40,48},{48,56},{56,0},{1,9},... | collective-permute-start | bytes 126728 | tf_op jit(solution)/shard_map/ppermute | solution.py:21
  68.6 0.8 copy-done.10
  69.4 3.9 %collective-permute-done.2 = f32[5,2,8,132]{3,1,2,0:T(2,128)S(1)} collective-permute-done((f32[5,2,8,132]{3,1,2,0:T(2,128)S(1)}, f32[5,2,8,132]{3,1,2,0:T(2,128)S(1)}, u32[]{:S(2)}, u32[]{:S(2)}) %collective-permute-start.2) | collective-permute-done | bytes 42272 | tf_op jit(solution)/shard_map/ppermute | solution.py:21
  73.3 0.9 pad_maximum_fusion.29
  74.2 4.8 %collective-permute-start.7 = (f32[5,20,2,132]{3,1,2,0:T(8,128)}, f32[5,20,2,132]{3,1,2,0:T(8,128)}, u32[]{:S(2)}, u32[]{:S(2)}) collective-permute-start(f32[5,20,2,132]{3,1,2,0:T(8,128)} %get-tuple-element.42), channel_id=1, source_target_pairs={{1,0},{2,1},{3,2},{4,3},{5,4},{6,5},{7,6},{0,7},{9,8},{10,9},{11,1... | collective-permute-start | bytes 316808 | tf_op jit(solution)/shard_map/ppermute | solution.py:22
  79.0 2.1 %collective-permute-start.6 = (f32[5,20,2,132]{3,1,2,0:T(8,128)S(1)}, f32[5,20,2,132]{3,1,2,0:T(8,128)S(1)}, u32[]{:S(2)}, u32[]{:S(2)}) collective-permute-start(f32[5,20,2,132]{3,1,2,0:T(8,128)S(1)} %get-tuple-element.41), channel_id=1, source_target_pairs={{0,1},{1,2},{2,3},{3,4},{4,5},{5,6},{6,7},{7,0},{8,9},{9,10},{10,1... | collective-permute-start | bytes 316808 | tf_op jit(solution)/shard_map/ppermute | solution.py:21
  81.7 0.6 copy-done.19
  82.7 0.7 collective-permute-done.7
  83.4 1.0 slice.684
  84.5 1.0 broadcast_select_fusion.7
  85.6 1.2 collective-permute-done.6
  87.1 0.8 copy-done.16
  87.9 0.9 copy-done.15
  89.0 1.0 copy-done.5
  90.0 0.8 fusion.23
  91.9 0.6 copy-done.2
  92.5 0.5 bitcast_add_fusion
  92.9 0.7 fusion.107
  93.8 5.1 %collective-permute-start.13 = (f32[5,16,8,2]{3,1,2,0:T(8,128)S(1)}, f32[5,16,8,2]{3,1,2,0:T(8,128)S(1)}, u32[]{:S(2)}, u32[]{:S(2)}) collective-permute-start(f32[5,16,8,2]{3,1,2,0:T(8,128)S(1)} %get-tuple-element.63), channel_id=1, source_target_pairs={{64,0},{128,64},{192,128},{256,192},{320,256},{384,320},{448,384},... | collective-permute-start | bytes 15368 | tf_op jit(solution)/shard_map/ppermute | solution.py:22
  99.0 0.9 rev.206
  99.9 1.9 %collective-permute-start.12 = (f32[5,16,8,2]{3,1,2,0:T(8,128)S(1)}, f32[5,16,8,2]{3,1,2,0:T(8,128)S(1)}, u32[]{:S(2)}, u32[]{:S(2)}) collective-permute-start(f32[5,16,8,2]{3,1,2,0:T(8,128)S(1)} %get-tuple-element.62), channel_id=1, source_target_pairs={{0,64},{64,128},{128,192},{192,256},{256,320},{320,384},{384,448},... | collective-permute-start | bytes 15368 | tf_op jit(solution)/shard_map/ppermute | solution.py:21
  102.1 1.4 collective-permute-done.13
  103.6 0.9 copy-done.3
  104.6 5.0 %collective-permute-done.12 = f32[5,16,8,2]{3,1,2,0:T(8,128)S(1)} collective-permute-done((f32[5,16,8,2]{3,1,2,0:T(8,128)S(1)}, f32[5,16,8,2]{3,1,2,0:T(8,128)S(1)}, u32[]{:S(2)}, u32[]{:S(2)}) %collective-permute-start.12) | collective-permute-done | bytes 5152 | tf_op jit(solution)/shard_map/ppermute | solution.py:21
  110.2 3.7 %collective-permute-start.15 = (f32[5,2,8,132]{3,1,2,0:T(2,128)S(1)}, f32[5,2,8,132]{3,1,2,0:T(2,128)S(1)}, u32[]{:S(2)}, u32[]{:S(2)}) collective-permute-start(f32[5,2,8,132]{3,1,2,0:T(2,128)S(1)} %get-tuple-element.44), channel_id=1, source_target_pairs={{8,0},{16,8},{24,16},{32,24},{40,32},{48,40},{56,48},{0,56},{9,1},... | collective-permute-start | bytes 126728 | tf_op jit(solution)/shard_map/ppermute | solution.py:22
  113.9 1.9 %collective-permute-start.14 = (f32[5,2,8,132]{3,1,2,0:T(2,128)S(1)}, f32[5,2,8,132]{3,1,2,0:T(2,128)S(1)}, u32[]{:S(2)}, u32[]{:S(2)}) collective-permute-start(f32[5,2,8,132]{3,1,2,0:T(2,128)S(1)} %get-tuple-element.43), channel_id=1, source_target_pairs={{0,8},{8,16},{16,24},{24,32},{32,40},{40,48},{48,56},{56,0},{1,9},... | collective-permute-start | bytes 126728 | tf_op jit(solution)/shard_map/ppermute | solution.py:21
  116.6 4.6 %collective-permute-done.14 = f32[5,2,8,132]{3,1,2,0:T(2,128)S(1)} collective-permute-done((f32[5,2,8,132]{3,1,2,0:T(2,128)S(1)}, f32[5,2,8,132]{3,1,2,0:T(2,128)S(1)}, u32[]{:S(2)}, u32[]{:S(2)}) %collective-permute-start.14) | collective-permute-done | bytes 42272 | tf_op jit(solution)/shard_map/ppermute | solution.py:21
  121.2 1.1 pad_maximum_fusion.24
  122.2 6.6 %collective-permute-start.17 = (f32[5,20,2,132]{3,1,2,0:T(8,128)}, f32[5,20,2,132]{3,1,2,0:T(8,128)S(1)}, u32[]{:S(2)}, u32[]{:S(2)}) collective-permute-start(f32[5,20,2,132]{3,1,2,0:T(8,128)} %get-tuple-element.40), channel_id=1, source_target_pairs={{1,0},{2,1},{3,2},{4,3},{5,4},{6,5},{7,6},{0,7},{9,8},{10,9},{11,1... | collective-permute-start | bytes 316808 | tf_op jit(solution)/shard_map/ppermute | solution.py:22
  128.9 3.3 %collective-permute-start.16 = (f32[5,20,2,132]{3,1,2,0:T(8,128)}, f32[5,20,2,132]{3,1,2,0:T(8,128)S(1)}, u32[]{:S(2)}, u32[]{:S(2)}) collective-permute-start(f32[5,20,2,132]{3,1,2,0:T(8,128)} %get-tuple-element.39), channel_id=1, source_target_pairs={{0,1},{1,2},{2,3},{3,4},{4,5},{5,6},{6,7},{7,0},{8,9},{9,10},{10,1... | collective-permute-start | bytes 316808 | tf_op jit(solution)/shard_map/ppermute | solution.py:21
  133.2 2.2 %collective-permute-done.17 = f32[5,20,2,132]{3,1,2,0:T(8,128)S(1)} collective-permute-done((f32[5,20,2,132]{3,1,2,0:T(8,128)}, f32[5,20,2,132]{3,1,2,0:T(8,128)S(1)}, u32[]{:S(2)}, u32[]{:S(2)}) %collective-permute-start.17) | collective-permute-done | bytes 105632 | tf_op jit(solution)/shard_map/ppermute | solution.py:22
  135.6 1.6 %collective-permute-done.16 = f32[5,20,2,132]{3,1,2,0:T(8,128)S(1)} collective-permute-done((f32[5,20,2,132]{3,1,2,0:T(8,128)}, f32[5,20,2,132]{3,1,2,0:T(8,128)S(1)}, u32[]{:S(2)}, u32[]{:S(2)}) %collective-permute-start.16) | collective-permute-done | bytes 105632 | tf_op jit(solution)/shard_map/ppermute | solution.py:21
  137.6 0.8 copy-done.18
  138.4 0.9 copy-done.17
  139.5 1.0 copy-done.7
  140.5 0.8 fusion.12
  142.5 0.8 copy.34
  (159 shorter events, 11.4 us)
Async XLA Ops:
  0.0 90.8 %copy-start = (f32[1,1,1,128,128]{4,3,2,1,0:T(8,128)S(1)}, f32[1,1,1,128,128]{4,3,2,1,0:T(8,128)}, u32[]{:S(2)}) copy-start(f32[1,1,1,128,128]{4,3,2,1,0:T(8,128)} %param.11) | copy-start | bytes 196612
  1.1 13.6 %copy-start.1 = (f32[9,16,8,128]{3,2,1,0:T(8,128)S(1)}, f32[9,16,8,128]{3,2,1,0:T(8,128)}, u32[]{:S(2)}) copy-start(f32[9,16,8,128]{3,2,1,0:T(8,128)} %param.7) | copy-start | bytes 1769476
  1.2 54.7 %collective-permute-start.1 = (f32[5,16,8,2]{3,1,2,0:T(8,128)S(1)}, f32[5,16,8,2]{3,1,2,0:T(8,128)S(1)}, u32[]{:S(2)}, u32[]{:S(2)}) collective-permute-start(f32[5,16,8,2]{3,1,2,0:T(8,128)S(1)} %get-tuple-element.71), channel_id=1, source_target_pairs={{64,0},{128,64},{192,128},{256,192},{320,256},{384,320},{448,384},... | collective-permute-start | bytes 15368 | tf_op jit(solution)/shard_map/ppermute | solution.py:22
  12.7 45.3 %collective-permute-start = (f32[5,16,8,2]{3,1,2,0:T(8,128)S(1)}, f32[5,16,8,2]{3,1,2,0:T(8,128)S(1)}, u32[]{:S(2)}, u32[]{:S(2)}) collective-permute-start(f32[5,16,8,2]{3,1,2,0:T(8,128)S(1)} %get-tuple-element.70), channel_id=1, source_target_pairs={{0,64},{64,128},{128,192},{192,256},{256,320},{320,384},{384,448},... | collective-permute-start | bytes 15368 | tf_op jit(solution)/shard_map/ppermute | solution.py:21
  16.1 20.9 %collective-permute-start.10 = (f32[3,16,8,1]{3,1,2,0:T(8,128)}, f32[3,16,8,1]{3,1,2,0:T(8,128)}, u32[]{:S(2)}, u32[]{:S(2)}) collective-permute-start(f32[3,16,8,1]{3,1,2,0:T(8,128)} %copy.48), channel_id=1, source_target_pairs={{0,64},{64,128},{128,192},{192,256},{256,320},{320,384},{384,448},... | collective-permute-start | bytes 4616 | tf_op jit(solution)/shard_map/ppermute | solution.py:21
  18.7 49.7 %collective-permute-start.9 = (f32[3,16,1,128]{3,1,2,0:T(8,128)S(1)}, f32[3,16,1,128]{3,1,2,0:T(8,128)S(1)}, u32[]{:S(2)}, u32[]{:S(2)}) collective-permute-start(f32[3,16,1,128]{3,1,2,0:T(8,128)S(1)} %bitcast.59), channel_id=1, source_target_pairs={{1,0},{2,1},{3,2},{4,3},{5,4},{6,5},{7,6},{0,7},{9,8},{10,9},{11,1... | collective-permute-start | bytes 73736 | tf_op jit(solution)/shard_map/ppermute | solution.py:22
  21.5 46.9 %collective-permute-start.8 = (f32[3,16,1,128]{3,1,2,0:T(8,128)}, f32[3,16,1,128]{3,1,2,0:T(8,128)S(1)}, u32[]{:S(2)}, u32[]{:S(2)}) collective-permute-start(f32[3,16,1,128]{3,1,2,0:T(8,128)} %bitcast.33), channel_id=1, source_target_pairs={{0,1},{1,2},{2,3},{3,4},{4,5},{5,6},{6,7},{7,0},{8,9},{9,10},{10,1... | collective-permute-start | bytes 73736 | tf_op jit(solution)/shard_map/ppermute | solution.py:21
  26.3 0.7 copy-start.21
  38.0 1.0 copy-start.12
  39.8 5.8 %copy-start.9 = (f32[3,16,8,128]{3,2,1,0:T(8,128)S(1)}, f32[3,16,8,128]{3,2,1,0:T(8,128)}, u32[]{:S(2)}) copy-start(f32[3,16,8,128]{3,2,1,0:T(8,128)} %get-tuple-element.49) | copy-start | bytes 589828
  39.8 8.7 %collective-permute-start.11 = (f32[3,16,8,1]{3,1,2,0:T(8,128)}, f32[3,16,8,1]{3,1,2,0:T(8,128)S(1)}, u32[]{:S(2)}, u32[]{:S(2)}) collective-permute-start(f32[3,16,8,1]{3,1,2,0:T(8,128)} %get-tuple-element.73), channel_id=1, source_target_pairs={{64,0},{128,64},{192,128},{256,192},{320,256},{384,320},{448,384},... | collective-permute-start | bytes 4616 | tf_op jit(solution)/shard_map/ppermute | solution.py:22
  45.7 1.0 copy-start.8
  48.5 17.3 %collective-permute-start.5 = (f32[3,1,8,128]{3,1,2,0:T(1,128)}, f32[3,1,8,128]{3,1,2,0:T(1,128)S(1)}, u32[]{:S(2)}, u32[]{:S(2)}) collective-permute-start(f32[3,1,8,128]{3,1,2,0:T(1,128)} %bitcast.32), channel_id=1, source_target_pairs={{8,0},{16,8},{24,16},{32,24},{40,32},{48,40},{56,48},{0,56},{9,1},... | collective-permute-start | bytes 36872 | tf_op jit(solution)/shard_map/ppermute | solution.py:22
  54.7 0.9 copy-start.13
  54.7 1.0 copy-start.14
  55.9 12.1 %collective-permute-start.4 = (f32[3,1,8,128]{3,1,2,0:T(1,128)}, f32[3,1,8,128]{3,1,2,0:T(1,128)S(1)}, u32[]{:S(2)}, u32[]{:S(2)}) collective-permute-start(f32[3,1,8,128]{3,1,2,0:T(1,128)} %bitcast.31), channel_id=1, source_target_pairs={{0,8},{8,16},{16,24},{24,32},{32,40},{40,48},{48,56},{56,0},{1,9},... | collective-permute-start | bytes 36872 | tf_op jit(solution)/shard_map/ppermute | solution.py:21
  58.7 10.7 %collective-permute-start.3 = (f32[5,2,8,132]{3,1,2,0:T(2,128)S(1)}, f32[5,2,8,132]{3,1,2,0:T(2,128)S(1)}, u32[]{:S(2)}, u32[]{:S(2)}) collective-permute-start(f32[5,2,8,132]{3,1,2,0:T(2,128)S(1)} %get-tuple-element.46), channel_id=1, source_target_pairs={{8,0},{16,8},{24,16},{32,24},{40,32},{48,40},{56,48},{0,56},{9,1},... | collective-permute-start | bytes 126728 | tf_op jit(solution)/shard_map/ppermute | solution.py:22
  65.0 0.9 copy-start.4
  65.8 2.4 %copy-start.11 = (f32[3,16,8,128]{3,1,2,0:T(8,128)S(1)}, f32[3,16,8,128]{3,1,2,0:T(8,128)}, u32[]{:S(2)}) copy-start(f32[3,16,8,128]{3,1,2,0:T(8,128)} %copy.44) | copy-start | bytes 589828
  65.8 7.4 %collective-permute-start.2 = (f32[5,2,8,132]{3,1,2,0:T(2,128)S(1)}, f32[5,2,8,132]{3,1,2,0:T(2,128)S(1)}, u32[]{:S(2)}, u32[]{:S(2)}) collective-permute-start(f32[5,2,8,132]{3,1,2,0:T(2,128)S(1)} %get-tuple-element.45), channel_id=1, source_target_pairs={{0,8},{8,16},{16,24},{24,32},{32,40},{40,48},{48,56},{56,0},{1,9},... | collective-permute-start | bytes 126728 | tf_op jit(solution)/shard_map/ppermute | solution.py:21
  68.5 0.9 copy-start.10
  74.2 9.2 %collective-permute-start.7 = (f32[5,20,2,132]{3,1,2,0:T(8,128)}, f32[5,20,2,132]{3,1,2,0:T(8,128)}, u32[]{:S(2)}, u32[]{:S(2)}) collective-permute-start(f32[5,20,2,132]{3,1,2,0:T(8,128)} %get-tuple-element.42), channel_id=1, source_target_pairs={{1,0},{2,1},{3,2},{4,3},{5,4},{6,5},{7,6},{0,7},{9,8},{10,9},{11,1... | collective-permute-start | bytes 316808 | tf_op jit(solution)/shard_map/ppermute | solution.py:22
  79.0 7.8 %collective-permute-start.6 = (f32[5,20,2,132]{3,1,2,0:T(8,128)S(1)}, f32[5,20,2,132]{3,1,2,0:T(8,128)S(1)}, u32[]{:S(2)}, u32[]{:S(2)}) collective-permute-start(f32[5,20,2,132]{3,1,2,0:T(8,128)S(1)} %get-tuple-element.41), channel_id=1, source_target_pairs={{0,1},{1,2},{2,3},{3,4},{4,5},{5,6},{6,7},{7,0},{8,9},{9,10},{10,1... | collective-permute-start | bytes 316808 | tf_op jit(solution)/shard_map/ppermute | solution.py:21
  81.5 0.8 copy-start.19
  87.0 0.9 copy-start.16
  87.9 0.9 copy-start.15
  88.9 1.1 copy-start.5
  90.8 0.7 copy-start.22
  91.5 1.0 copy-start.2
  91.5 1.0 copy-start.20
  93.8 9.7 %collective-permute-start.13 = (f32[5,16,8,2]{3,1,2,0:T(8,128)S(1)}, f32[5,16,8,2]{3,1,2,0:T(8,128)S(1)}, u32[]{:S(2)}, u32[]{:S(2)}) collective-permute-start(f32[5,16,8,2]{3,1,2,0:T(8,128)S(1)} %get-tuple-element.63), channel_id=1, source_target_pairs={{64,0},{128,64},{192,128},{256,192},{320,256},{384,320},{448,384},... | collective-permute-start | bytes 15368 | tf_op jit(solution)/shard_map/ppermute | solution.py:22
  99.9 9.7 %collective-permute-start.12 = (f32[5,16,8,2]{3,1,2,0:T(8,128)S(1)}, f32[5,16,8,2]{3,1,2,0:T(8,128)S(1)}, u32[]{:S(2)}, u32[]{:S(2)}) collective-permute-start(f32[5,16,8,2]{3,1,2,0:T(8,128)S(1)} %get-tuple-element.62), channel_id=1, source_target_pairs={{0,64},{64,128},{128,192},{192,256},{256,320},{320,384},{384,448},... | collective-permute-start | bytes 15368 | tf_op jit(solution)/shard_map/ppermute | solution.py:21
  103.5 1.0 copy-start.3
  110.2 6.4 %collective-permute-start.15 = (f32[5,2,8,132]{3,1,2,0:T(2,128)S(1)}, f32[5,2,8,132]{3,1,2,0:T(2,128)S(1)}, u32[]{:S(2)}, u32[]{:S(2)}) collective-permute-start(f32[5,2,8,132]{3,1,2,0:T(2,128)S(1)} %get-tuple-element.44), channel_id=1, source_target_pairs={{8,0},{16,8},{24,16},{32,24},{40,32},{48,40},{56,48},{0,56},{9,1},... | collective-permute-start | bytes 126728 | tf_op jit(solution)/shard_map/ppermute | solution.py:22
  113.9 7.3 %collective-permute-start.14 = (f32[5,2,8,132]{3,1,2,0:T(2,128)S(1)}, f32[5,2,8,132]{3,1,2,0:T(2,128)S(1)}, u32[]{:S(2)}, u32[]{:S(2)}) collective-permute-start(f32[5,2,8,132]{3,1,2,0:T(2,128)S(1)} %get-tuple-element.43), channel_id=1, source_target_pairs={{0,8},{8,16},{16,24},{24,32},{32,40},{40,48},{48,56},{56,0},{1,9},... | collective-permute-start | bytes 126728 | tf_op jit(solution)/shard_map/ppermute | solution.py:21
  116.6 5.6 %copy-start.6 = (f32[5,16,8,130]{3,1,2,0:T(8,128)}, f32[5,16,8,130]{3,1,2,0:T(8,128)S(1)}, u32[]{:S(2)}) copy-start(f32[5,16,8,130]{3,1,2,0:T(8,128)S(1)} %multiply_dynamic-update-slice_fusion) | copy-start | bytes 998404
  122.2 13.1 %collective-permute-start.17 = (f32[5,20,2,132]{3,1,2,0:T(8,128)}, f32[5,20,2,132]{3,1,2,0:T(8,128)S(1)}, u32[]{:S(2)}, u32[]{:S(2)}) collective-permute-start(f32[5,20,2,132]{3,1,2,0:T(8,128)} %get-tuple-element.40), channel_id=1, source_target_pairs={{1,0},{2,1},{3,2},{4,3},{5,4},{6,5},{7,6},{0,7},{9,8},{10,9},{11,1... | collective-permute-start | bytes 316808 | tf_op jit(solution)/shard_map/ppermute | solution.py:22
  128.9 8.4 %collective-permute-start.16 = (f32[5,20,2,132]{3,1,2,0:T(8,128)}, f32[5,20,2,132]{3,1,2,0:T(8,128)S(1)}, u32[]{:S(2)}, u32[]{:S(2)}) collective-permute-start(f32[5,20,2,132]{3,1,2,0:T(8,128)} %get-tuple-element.39), channel_id=1, source_target_pairs={{0,1},{1,2},{2,3},{3,4},{4,5},{5,6},{6,7},{7,0},{8,9},{9,10},{10,1... | collective-permute-start | bytes 316808 | tf_op jit(solution)/shard_map/ppermute | solution.py:21
  137.5 0.9 copy-start.18
  138.3 0.9 copy-start.17
  139.4 1.1 copy-start.7
where the time goes:
time: 145 us; the launch traced here: 143 us
  starting transfers between devices  72.1 us (50%)
  local copies, waits for them, and re-layouts  27.6 us (19%)
  waiting for transfers between devices  21 us (14%)
  other arithmetic  11.1 us (8%)
  between operations  8.89 us (6%)
  matrix products  2.6 us (2%)
    ppermute x9, starting transfers between devices, padded_2(): after = lax.ppermute(leading, axis, down)  51 us
    ppermute x9, starting transfers between devices, padded_2(): before = lax.ppermute(last, axis, up)  21.1 us
    ppermute x9, waiting for transfers between devices, padded_2(): before = lax.ppermute(last, axis, up)  16.2 us
    unnamed x51, local copies, waits for them, and re-layouts  15 us
    ppermute x9, waiting for transfers between devices, padded_2(): after = lax.ppermute(leading, axis, down)  4.71 us
  transfers between devices with their start and end apart: 18, of which 9 were waited for; matrix products, arithmetic and copies ran while one was open for 14% of the time, Pallas kernels for 0%

commit v1 on v0

v1 whole, which is shorter than its diff:
```python
import functools

import jax
import jax.numpy as jnp
from jax import lax
from jax.experimental import pallas as pl
from jax.experimental.pallas import tpu as pltpu
from jax.sharding import PartitionSpec as P

MESH = pl.DeviceIdType.MESH
HIGHEST = lax.Precision.HIGHEST
AXES = ("chord", "normal", "span")
SWEEPS = 2
FIELDS = 5
NI, NJ, NK = 16, 8, 128
CELLS = NI * NJ

gas_factor = 0.4
damping = 0.1
pseudo_step = 0.03


def dot(a, b, contract):
    return lax.dot_general(
        a, b, (contract, ((), ())), precision=HIGHEST, preferred_element_type=jnp.float32
    )


def thermo(g):
    inv = 1.0 / g[0]
    kinetic = 0.5 * (g[1] * g[1] + g[2] * g[2] + g[3] * g[3]) * inv
    pressure = gas_factor * (g[4] - kinetic)
    return inv, pressure


def flux(g, inv, pressure, n):
    speed = (n[0] * g[1] + n[1] * g[2] + n[2] * g[3]) * inv
    return [
        g[0] * speed,
        g[1] * speed + n[0] * pressure,
        g[2] * speed + n[1] * pressure,
        g[3] * speed + n[2] * pressure,
        (g[4] + pressure) * speed,
    ]


def face_terms(edge, behind, n, half):
    inv, pressure = thermo(edge)
    f = flux(edge, inv, pressure, n)
    send, keep, far = [], [], []
    for v in range(FIELDS):
        smooth = 4.0 * damping * edge[v] - damping * behind[v]
        send.append(smooth + half * f[v])
        keep.append(smooth - half * f[v])
        far.append(-damping * edge[v])
    return send, keep, far


def lanes(x, index):
    return jnp.take_along_axis(x, index, axis=1, mode="promise_in_bounds")


def rows(x, index):
    return jnp.take_along_axis(x, index, axis=0, mode="promise_in_bounds")


def kernel(
    codes, state, metrics, inv_i, inv_j, inv_k, out,
    u, n, r, gi, t, m_ij, n_k,
    send_i, send_j, send_k, keep_i, keep_j, keep_k, recv_i, recv_j, recv_k,
    load_sem, send_sem, recv_sem,
):
    load_u = pltpu.make_async_copy(state, u.at[:, pl.ds(2 * NJ, CELLS), :], load_sem.at[0])
    load_n = pltpu.make_async_copy(metrics, n, load_sem.at[1])
    load_u.start()
    load_n.start()

    near = []
    for axis in AXES:
        size, me = lax.axis_size(axis), lax.axis_index(axis)
        near.append((lax.rem(me + size - 1, size), lax.rem(me + 1, size)))
    barrier = pltpu.get_barrier_semaphore()
    for d, axis in enumerate(AXES):
        for side in range(2):
            pl.semaphore_signal(
                barrier, inc=1, device_id={axis: near[d][side]}, device_id_type=MESH
            )

    sends = (send_i, send_j, send_k)
    recvs = (recv_i, recv_j, recv_k)

    def copy(sweep, d, side):
        return pltpu.make_async_remote_copy(
            src_ref=sends[d].at[sweep, side],
            dst_ref=recvs[d].at[sweep, 1 - side],
            send_sem=send_sem.at[sweep, d, side],
            recv_sem=recv_sem.at[sweep, d, 1 - side],
            device_id={AXES[d]: near[d][side]},
            device_id_type=MESH,
        )

    copies = [[[copy(s, d, side) for side in range(2)] for d in range(3)] for s in range(SWEEPS)]

    sub = lax.broadcasted_iota(jnp.int32, (8, NK), 0)
    lane = lax.broadcasted_iota(jnp.int32, (8, NK), 1)
    low4 = jnp.bitwise_and(sub, 3)
    picked = jnp.where(
        low4 == 0, 0, jnp.where(low4 == 1, NK - 1, jnp.where(low4 == 2, 1, NK - 2))
    )
    pick = jnp.where(lane == picked, 1.0, 0.0).astype(jnp.float32)
    place = jnp.where(sub < 4, pick, 0.0)
    even = jnp.bitwise_and(sub, 1) == 0
    lane_rev = NK - 1 - lane
    row_rev = 7 - sub
    lane_rev_i = jnp.bitwise_xor(lane, CELLS - NJ)
    lane_rev_j = jnp.bitwise_xor(lane, NJ - 1)

    code = [jnp.full((8, NK), codes[0, q], jnp.int32) for q in range(6)]
    bit0 = [jnp.bitwise_and(c - 1, 1) == 1 for c in code]
    bit1 = [jnp.bitwise_and(c - 1, 2) == 2 for c in code]
    joined = [c > 0 for c in code]

    zero = jnp.zeros((2 * NJ, NK), jnp.float32)
    for v in range(FIELDS):
        u[v, pl.ds(0, 2 * NJ), :] = zero
        u[v, pl.ds(2 * NJ + CELLS, 2 * NJ), :] = zero
        gi[v, pl.ds(0, NJ), :] = zero[:NJ]
        gi[v, pl.ds(NJ + CELLS, NJ), :] = zero[:NJ]

    load_u.wait()
    load_n.wait()

    def edge_i(sweep):
        for side in range(2):
            at = 0 if side == 0 else NI - 1
            back = 1 if side == 0 else NI - 2
            edge = [u[v, pl.ds((2 + at) * NJ, NJ), :] for v in range(FIELDS)]
            behind = [u[v, pl.ds((2 + back) * NJ, NJ), :] for v in range(FIELDS)]
            nn = [n[c, pl.ds(at * NJ, NJ), :] for c in range(3)]
            send, keep, far = face_terms(edge, behind, nn, -0.5 if side == 0 else 0.5)
            for v in range(FIELDS):
                send_i[sweep, side, v] = send[v]
                send_i[sweep, side, FIELDS + v] = far[v]
                keep_i[side, v] = keep[v]

    def edge_j(sweep):
        for side in range(2):
            at = 0 if side == 0 else NJ - 1
            back = 1 if side == 0 else NJ - 2
            edge = [u[v, pl.ds(2 * NJ + at, NI, stride=NJ), :] for v in range(FIELDS)]
            behind = [u[v, pl.ds(2 * NJ + back, NI, stride=NJ), :] for v in range(FIELDS)]
            nn = [n[3 + c, pl.ds(at, NI, stride=NJ), :] for c in range(3)]
            send, keep, far = face_terms(edge, behind, nn, -0.5 if side == 0 else 0.5)
            for v in range(FIELDS):
                send_j[sweep, side, v] = send[v]
                send_j[sweep, side, FIELDS + v] = far[v]
                keep_j[side, v] = keep[v]

    def edge_k(sweep):
        edge = [dot(pick, u[v, pl.ds(2 * NJ, CELLS), :], ((1,), (1,))) for v in range(FIELDS)]
        behind = [pltpu.roll(e, 6, 0) for e in edge]
        nn = [n_k[c] for c in range(3)]
        half = jnp.where(even, -0.5, 0.5)
        send, keep, far = face_terms(edge, behind, nn, half)
        for v in range(FIELDS):
            far_rows = pltpu.roll(far[v], 2, 0)
            send_k[sweep, 0, v] = jnp.where(sub < 2, send[v], far_rows)
            send_k[sweep, 1, v] = jnp.where(sub < 2, send[v], far_rows)
            keep_k[v] = jnp.where(sub < 2, keep[v], far_rows)

    def interior():
        first_j, last_j = sub == 0, sub == NJ - 1
        first_k, last_k = lane == 0, lane == NK - 1

        def slab(i, carry):
            at = pl.multiple_of(i * NJ, NJ)
            g = [u[v, pl.ds(2 * NJ + at, NJ), :] for v in range(FIELDS)]
            nn = [n[c, pl.ds(at, NJ), :] for c in range(9)]
            inv, pressure = thermo(g)
            f = flux(g, inv, pressure, nn[0:3])
            for v in range(FIELDS):
                gi[v, pl.ds(NJ + at, NJ), :] = 0.5 * f[v]
            total = [-18.0 * damping * g[v] for v in range(FIELDS)]
            for d, axis, length, first, last in (
                (1, 0, NJ, first_j, last_j), (2, 1, NK, first_k, last_k),
            ):
                f = flux(g, inv, pressure, nn[3 * d : 3 * d + 3])
                for v in range(FIELDS):
                    def above(x):
                        return jnp.where(last, 0.0, pltpu.roll(x, length - 1, axis))

                    def below(x):
                        return jnp.where(first, 0.0, pltpu.roll(x, 1, axis))

                    smooth, half = 4.0 * damping * g[v], 0.5 * f[v]
                    up = smooth - half - damping * above(g[v])
                    down = smooth + half - damping * below(g[v])
                    total[v] = total[v] + above(up) + below(down)
            for v in range(FIELDS):
                r[v, pl.ds(at, NJ), :] = total[v]
            return carry

        lax.fori_loop(0, NI, slab, 0)

        def chord(i, carry):
            at = pl.multiple_of(i * NJ, NJ)
            for v in range(FIELDS):
                layer = [u[v, pl.ds(at + q * NJ, NJ), :] for q in (0, 1, 3, 4)]
                r[v, pl.ds(at, NJ), :] = (
                    r[v, pl.ds(at, NJ), :]
                    + gi[v, pl.ds(at, NJ), :]
                    - gi[v, pl.ds(at + 2 * NJ, NJ), :]
                    + 4.0 * damping * (layer[1] + layer[2])
                    - damping * (layer[0] + layer[3])
                )
            return carry

        lax.fori_loop(0, NI, chord, 0)

    def halo_k(sweep):
        for side in range(2):
            copies[sweep][2][1 - side].wait_recv()
        lo, hi = 4, 5
        flip_i = jnp.where(even, bit0[lo].astype(jnp.int32), bit0[hi].astype(jnp.int32)) == 1
        flip_j = jnp.where(even, bit1[lo].astype(jnp.int32), bit1[hi].astype(jnp.int32)) == 1
        linked = jnp.where(even, code[lo], code[hi]) > 0
        for v in range(FIELDS):
            z = jnp.where(
                even, pltpu.roll(recv_k[sweep, 0, v], 7, 0), pltpu.roll(recv_k[sweep, 1, v], 1, 0)
            )
            z = jnp.where(flip_i, lanes(z, lane_rev_i), z)
            z = jnp.where(flip_j, lanes(z, lane_rev_j), z)
            z = jnp.where(linked, z, keep_k[v])
            r[v] = r[v] + dot(z, place, ((0,), (0,)))

    def halo_i(sweep):
        for side in range(2):
            copies[sweep][0][1 - side].wait_recv()
            face = side
            for q in range(2 * FIELDS):
                v = q % FIELDS
                x = recv_i[sweep, side, q]
                x = jnp.where(bit0[face], rows(x, row_rev), x)
                x = jnp.where(bit1[face], lanes(x, lane_rev), x)
                own = keep_i[side, v] if q < FIELDS else send_i[sweep, side, q]
                x = jnp.where(joined[face], x, own)
                depth = 0 if q < FIELDS else 1
                at = (depth if side == 0 else NI - 1 - depth) * NJ
                r[v, pl.ds(at, NJ), :] = r[v, pl.ds(at, NJ), :] + x

    def halo_j(sweep):
        for side in range(2):
            copies[sweep][1][1 - side].wait_recv()
            face = 2 + side
            for q in range(2 * FIELDS):
                v = q % FIELDS
                x = [recv_j[sweep, side, q, pl.ds(8 * h, 8), :] for h in range(2)]
                rev = [rows(x[1 - h], row_rev) for h in range(2)]
                x = [jnp.where(bit0[face], rev[h], x[h]) for h in range(2)]
                x = [jnp.where(bit1[face], lanes(x[h], lane_rev), x[h]) for h in range(2)]
                depth = 0 if q < FIELDS else 1
                at = depth if side == 0 else NJ - 1 - depth
                for h in range(2):
                    part = pl.ds(8 * h, 8)
                    own = keep_j[side, v, part, :] if q < FIELDS else send_j[sweep, side, q, part, :]
                    y = jnp.where(joined[face], x[h], own)
                    where = pl.ds(8 * h * NJ + at, 8, stride=NJ)
                    r[v, where, :] = r[v, where, :] + y

    def solve(sweep):
        for v in range(FIELDS):
            t[v] = dot(r[v], inv_k[...], ((1,), (1,)))
        for v in range(FIELDS):
            change = dot(m_ij[...], t[v], ((1,), (0,)))
            if sweep == 0:
                out[v] = change
                inner = pl.ds(2 * NJ, CELLS)
                u[v, inner, :] = u[v, inner, :] + pseudo_step * change
            else:
                out[v] = out[v] + change

    for sweep in range(SWEEPS):
        edge_j(sweep)
        if sweep == 0:
            pl.semaphore_wait(barrier, 6)
        for side in range(2):
            copies[sweep][1][side].start()
        edge_i(sweep)
        for side in range(2):
            copies[sweep][0][side].start()
        if sweep == 0:
            for c in range(3):
                n_k[c] = dot(pick, n[6 + c], ((1,), (1,)))
        edge_k(sweep)
        for side in range(2):
            copies[sweep][2][side].start()
        interior()
        if sweep == 0:
            wide = lax.broadcasted_iota(jnp.int32, (CELLS, NI), 0)
            e_i = jnp.where(
                lax.shift_right_logical(wide, 3)
                == lax.broadcasted_iota(jnp.int32, (CELLS, NI), 1), 1.0, 0.0,
            ).astype(jnp.float32)
            wide = lax.broadcasted_iota(jnp.int32, (CELLS, NJ), 0)
            e_j = jnp.where(
                jnp.bitwise_and(wide, 7) == lax.broadcasted_iota(jnp.int32, (CELLS, NJ), 1), 1.0, 0.0
            ).astype(jnp.float32)
            big_i = dot(dot(e_i, inv_i[...], ((1,), (0,))), e_i, ((1,), (1,)))
            big_j = dot(dot(e_j, inv_j[...], ((1,), (0,))), e_j, ((1,), (1,)))
            m_ij[...] = big_i * big_j
        halo_k(sweep)
        halo_i(sweep)
        halo_j(sweep)
        solve(sweep)

    for sweep in range(SWEEPS):
        for d in range(3):
            for side in range(2):
                copies[sweep][d][side].wait_send()


def local(state, metrics, face_codes, inverse_i, inverse_j, inverse_k):
    f32 = jnp.float32
    vmem = pl.BlockSpec(memory_space=pltpu.VMEM)
    anywhere = pl.BlockSpec(memory_space=pl.ANY)
    result = pl.pallas_call(
        kernel,
        out_shape=jax.ShapeDtypeStruct((FIELDS, CELLS, NK), f32),
        in_specs=[pl.BlockSpec(memory_space=pltpu.SMEM), anywhere, anywhere, vmem, vmem, vmem],
        out_specs=vmem,
        scratch_shapes=[
            pltpu.VMEM((FIELDS, CELLS + 4 * NJ, NK), f32),
            pltpu.VMEM((9, CELLS, NK), f32),
            pltpu.VMEM((FIELDS, CELLS, NK), f32),
            pltpu.VMEM((FIELDS, CELLS + 2 * NJ, NK), f32),
            pltpu.VMEM((FIELDS, CELLS, NK), f32),
            pltpu.VMEM((CELLS, CELLS), f32),
            pltpu.VMEM((3, 8, NK), f32),
            pltpu.VMEM((SWEEPS, 2, 2 * FIELDS, NJ, NK), f32),
            pltpu.VMEM((SWEEPS, 2, 2 * FIELDS, NI, NK), f32),
            pltpu.VMEM((SWEEPS, 2, FIELDS, 8, NK), f32),
            pltpu.VMEM((2, FIELDS, NJ, NK), f32),
            pltpu.VMEM((2, FIELDS, NI, NK), f32),
            pltpu.VMEM((FIELDS, 8, NK), f32),
            pltpu.VMEM((SWEEPS, 2, 2 * FIELDS, NJ, NK), f32),
            pltpu.VMEM((SWEEPS, 2, 2 * FIELDS, NI, NK), f32),
            pltpu.VMEM((SWEEPS, 2, FIELDS, 8, NK), f32),
            pltpu.SemaphoreType.DMA((2,)),
            pltpu.SemaphoreType.DMA((SWEEPS, 3, 2)),
            pltpu.SemaphoreType.DMA((SWEEPS, 3, 2)),
        ],
        compiler_params=pltpu.CompilerParams(collective_id=0, has_side_effects=True),
        name="adi",
    )(
        face_codes.reshape(1, 6),
        state.reshape(FIELDS, CELLS, NK),
        metrics.reshape(9, CELLS, NK),
        inverse_i.reshape(NI, NI),
        inverse_j.reshape(NJ, NJ),
        inverse_k.reshape(NK, NK),
    )
    return result.reshape(state.shape)


def solution(mesh):
    cells = P(None, "chord", "normal", "span")
    block = P("chord", "normal", "span", None, None)
    return jax.shard_map(
        local,
        mesh=mesh,
        in_specs=(cells, cells, P("chord", "normal", "span", None), block, block, block),
        out_specs=cells,
        check_vma=False,
    )
```

time: 145 us -> 30.3 us (0.21)
  the two profiles are of different devices: /device:TPU:1 before, /device:TPU:16 now
where the time goes in v1:
time: 30.3 us; the launch traced here: 30.1 us
  Pallas kernels  28.4 us (94%)
  local copies, waits for them, and re-layouts  1.72 us (6%)
    pallas_call x1, Pallas kernels, local(): pl.pallas_call(kernel, out_shape=jax.ShapeDtypeStruct((FIELDS, CELLS, NK)...  28.4 us
    unnamed x1, local copies, waits for them, and re-layouts  1.72 us

profile of v1, /device:TPU:16, one launch (start us, length us, event | category | flops | bytes accessed | tf_op | source)
XLA Modules:
  0.0 30.1 jit_solution(4079195784300389153)
XLA Ops:
  0.0 28.4 %adi.1 = f32[5,128,128]{2,1,0:T(8,128)} custom-call(s32[1,6]{1,0:T(1,128)} %bitcast.13, f32[5,128,128]{2,1,0:T(8,128)} %bitcast.9, f32[9,128,128]{2,1,0:T(8,128)} %bitcast.8, f32[16,16]{1,0:T(8,128)} %bitcast.11, f32[8,8]{1,0:T(8,128)} %bitcast.12, f32[128,128]{1,0:T(8,128)} %bitcast.10), custom_call_target="tpu_custom_call" | custom-call | tf_op jit(solution)/shard_map/adi/pallas_call | solution.py:326
  28.4 1.7 %copy.8 = f32[5,16,8,128]{3,2,1,0:T(8,128)} copy(f32[5,16,8,128]{3,2,1,0:T(8,128)} %bitcast.7) | data formatting | bytes 655360

commit v2 on v1

--- a/solution.py
+++ b/solution.py
@@ -9,6 +9,7 @@
 
 MESH = pl.DeviceIdType.MESH
 HIGHEST = lax.Precision.HIGHEST
+BF16 = jnp.bfloat16
 AXES = ("chord", "normal", "span")
 SWEEPS = 2
 FIELDS = 5
@@ -56,6 +57,18 @@
     return send, keep, far
 
 
+def halves(x):
+    high = x.astype(BF16)
+    return high, (x - high.astype(jnp.float32)).astype(BF16)
+
+
+def product(a, b):
+    both = lax.dot_general(
+        a, b, (((1,), (0,)), ((), ())), preferred_element_type=jnp.float32
+    )
+    return both[:, :NK] + both[:, NK:]
+
+
 def lanes(x, index):
     return jnp.take_along_axis(x, index, axis=1, mode="promise_in_bounds")
 
@@ -65,15 +78,23 @@
 
 
 def kernel(
-    codes, state, metrics, inv_i, inv_j, inv_k, out,
-    u, n, r, gi, t, m_ij, n_k,
+    codes_hbm, state, metrics, inv_i_hbm, inv_j_hbm, inv_k_hbm, out,
+    codes, u, n, inv_i, inv_j, inv_k, r, gi, r2, w_k, m2, cross, n_k,
     send_i, send_j, send_k, keep_i, keep_j, keep_k, recv_i, recv_j, recv_k,
     load_sem, send_sem, recv_sem,
 ):
     load_u = pltpu.make_async_copy(state, u.at[:, pl.ds(2 * NJ, CELLS), :], load_sem.at[0])
     load_n = pltpu.make_async_copy(metrics, n, load_sem.at[1])
+    load_rest = [
+        pltpu.make_async_copy(a, b, load_sem.at[2 + q])
+        for q, (a, b) in enumerate((
+            (codes_hbm, codes), (inv_i_hbm, inv_i), (inv_j_hbm, inv_j), (inv_k_hbm, inv_k),
+        ))
+    ]
     load_u.start()
     load_n.start()
+    for load in load_rest:
+        load.start()
 
     near = []
     for axis in AXES:
@@ -91,7 +112,7 @@
 
     def copy(sweep, d, side):
         return pltpu.make_async_remote_copy(
-            src_ref=sends[d].at[sweep, side],
+            src_ref=sends[d].at[sweep] if d == 2 else sends[d].at[sweep, side],
             dst_ref=recvs[d].at[sweep, 1 - side],
             send_sem=send_sem.at[sweep, d, side],
             recv_sem=recv_sem.at[sweep, d, 1 - side],
@@ -103,22 +124,21 @@
 
     sub = lax.broadcasted_iota(jnp.int32, (8, NK), 0)
     lane = lax.broadcasted_iota(jnp.int32, (8, NK), 1)
-    low4 = jnp.bitwise_and(sub, 3)
-    picked = jnp.where(
-        low4 == 0, 0, jnp.where(low4 == 1, NK - 1, jnp.where(low4 == 2, 1, NK - 2))
-    )
-    pick = jnp.where(lane == picked, 1.0, 0.0).astype(jnp.float32)
-    place = jnp.where(sub < 4, pick, 0.0)
-    even = jnp.bitwise_and(sub, 1) == 0
     lane_rev = NK - 1 - lane
     row_rev = 7 - sub
+    row_swap = jnp.where(sub < 4, 3 - sub, sub)
+    outer_k = jnp.logical_or(sub == 1, sub == 2)
+    top_k = sub < 2
+    last_k4 = jnp.logical_or(lane < 2, lane >= NK - 2)
     lane_rev_i = jnp.bitwise_xor(lane, CELLS - NJ)
     lane_rev_j = jnp.bitwise_xor(lane, NJ - 1)
 
-    code = [jnp.full((8, NK), codes[0, q], jnp.int32) for q in range(6)]
-    bit0 = [jnp.bitwise_and(c - 1, 1) == 1 for c in code]
-    bit1 = [jnp.bitwise_and(c - 1, 2) == 2 for c in code]
-    joined = [c > 0 for c in code]
+    def read_codes():
+        code = [jnp.full((8, NK), codes[0, q], jnp.int32) for q in range(6)]
+        bit0 = [jnp.bitwise_and(c - 1, 1) == 1 for c in code]
+        bit1 = [jnp.bitwise_and(c - 1, 2) == 2 for c in code]
+        joined = [c > 0 for c in code]
+        return code, bit0, bit1, joined
 
     zero = jnp.zeros((2 * NJ, NK), jnp.float32)
     for v in range(FIELDS):
@@ -126,6 +146,7 @@
         u[v, pl.ds(2 * NJ + CELLS, 2 * NJ), :] = zero
         gi[v, pl.ds(0, NJ), :] = zero[:NJ]
         gi[v, pl.ds(NJ + CELLS, NJ), :] = zero[:NJ]
+    cross[...] = jnp.zeros((CELLS, NK), jnp.float32)
 
     load_u.wait()
     load_n.wait()
@@ -157,16 +178,26 @@
                 keep_j[side, v] = keep[v]
 
     def edge_k(sweep):
-        edge = [dot(pick, u[v, pl.ds(2 * NJ, CELLS), :], ((1,), (1,))) for v in range(FIELDS)]
-        behind = [pltpu.roll(e, 6, 0) for e in edge]
-        nn = [n_k[c] for c in range(3)]
-        half = jnp.where(even, -0.5, 0.5)
-        send, keep, far = face_terms(edge, behind, nn, half)
+        for i in range(NI):
+            x = [u[v, pl.ds((2 + i) * NJ, NJ), :] for v in range(FIELDS)]
+            if sweep == 0:
+                x = x + [n[6 + c, pl.ds(i * NJ, NJ), :] for c in range(3)]
+            y = pltpu.roll(x[0], 2, 1)
+            for v in range(1, len(x)):
+                y = jnp.where(lane >= 8 * v, pltpu.roll(x[v], 8 * v + 2, 1), y)
+            cross[pl.ds(i * NJ, NJ), :] = y
+        packed = jnp.transpose(cross[...])
+        if sweep == 0:
+            for c in range(3):
+                n_k[c] = packed[8 * (FIELDS + c) : 8 * (FIELDS + c) + 8]
+        edge = [packed[8 * v : 8 * v + 8] for v in range(FIELDS)]
+        behind = [jnp.where(top_k, pltpu.roll(e, 1, 0), pltpu.roll(e, 7, 0)) for e in edge]
+        half = jnp.where(top_k, 0.5, -0.5)
+        send, keep, far = face_terms(edge, behind, [n_k[c] for c in range(3)], half)
         for v in range(FIELDS):
-            far_rows = pltpu.roll(far[v], 2, 0)
-            send_k[sweep, 0, v] = jnp.where(sub < 2, send[v], far_rows)
-            send_k[sweep, 1, v] = jnp.where(sub < 2, send[v], far_rows)
-            keep_k[v] = jnp.where(sub < 2, keep[v], far_rows)
+            next_rows = jnp.where(top_k, pltpu.roll(far[v], 7, 0), pltpu.roll(far[v], 1, 0))
+            send_k[sweep, v] = rows(jnp.where(outer_k, send[v], next_rows), row_swap)
+            keep_k[v] = jnp.where(outer_k, keep[v], next_rows)
 
     def interior():
         first_j, last_j = sub == 0, sub == NJ - 1
@@ -220,18 +251,22 @@
     def halo_k(sweep):
         for side in range(2):
             copies[sweep][2][1 - side].wait_recv()
-        lo, hi = 4, 5
-        flip_i = jnp.where(even, bit0[lo].astype(jnp.int32), bit0[hi].astype(jnp.int32)) == 1
-        flip_j = jnp.where(even, bit1[lo].astype(jnp.int32), bit1[hi].astype(jnp.int32)) == 1
-        linked = jnp.where(even, code[lo], code[hi]) > 0
+        flip_i = jnp.bitwise_and(jnp.where(top_k, code[5], code[4]) - 1, 1) == 1
+        flip_j = jnp.bitwise_and(jnp.where(top_k, code[5], code[4]) - 1, 2) == 2
+        linked = jnp.where(top_k, code[5], code[4]) > 0
         for v in range(FIELDS):
-            z = jnp.where(
-                even, pltpu.roll(recv_k[sweep, 0, v], 7, 0), pltpu.roll(recv_k[sweep, 1, v], 1, 0)
-            )
+            z = jnp.where(top_k, recv_k[sweep, 1, v], recv_k[sweep, 0, v])
             z = jnp.where(flip_i, lanes(z, lane_rev_i), z)
             z = jnp.where(flip_j, lanes(z, lane_rev_j), z)
-            z = jnp.where(linked, z, keep_k[v])
-            r[v] = r[v] + dot(z, place, ((0,), (0,)))
+            cross[pl.ds(8 * v, 8), :] = jnp.where(linked, z, keep_k[v])
+        spread = jnp.transpose(cross[...])
+        for i in range(NI):
+            part = pl.ds(i * NJ, NJ)
+            x = spread[i * NJ : (i + 1) * NJ]
+            for v in range(FIELDS):
+                r[v, part, :] = r[v, part, :] + jnp.where(
+                    last_k4, pltpu.roll(x, NK - 2 - 8 * v, 1), 0.0
+                )
 
     def halo_i(sweep):
         for side in range(2):
@@ -267,11 +302,38 @@
                     where = pl.ds(8 * h * NJ + at, 8, stride=NJ)
                     r[v, where, :] = r[v, where, :] + y
 
+    def prepare():
+        for load in load_rest[1:]:
+            load.wait()
+        high, low = halves(jnp.transpose(inv_k[...]))
+        for h in range(2):
+            w_k[pl.ds(h * NK, NK), pl.ds(0, NK)] = high
+            w_k[pl.ds(h * NK, NK), pl.ds(NK, NK)] = low
+        wide = lax.broadcasted_iota(jnp.int32, (CELLS, NI), 0)
+        e_i = jnp.where(
+            lax.shift_right_logical(wide, 3)
+            == lax.broadcasted_iota(jnp.int32, (CELLS, NI), 1), 1.0, 0.0,
+        ).astype(jnp.float32)
+        wide = lax.broadcasted_iota(jnp.int32, (CELLS, NJ), 0)
+        e_j = jnp.where(
+            jnp.bitwise_and(wide, 7) == lax.broadcasted_iota(jnp.int32, (CELLS, NJ), 1), 1.0, 0.0
+        ).astype(jnp.float32)
+        big_i = dot(dot(e_i, inv_i[...], ((1,), (0,))), e_i, ((1,), (1,)))
+        big_j = dot(dot(e_j, inv_j[...], ((1,), (0,))), e_j, ((1,), (1,)))
+        high, low = halves(big_i * big_j)
+        m2[:, pl.ds(0, CELLS)] = high
+        m2[:, pl.ds(CELLS, CELLS)] = low
+
     def solve(sweep):
         for v in range(FIELDS):
-            t[v] = dot(r[v], inv_k[...], ((1,), (1,)))
+            high, low = halves(r[v])
+            r2[v, :, pl.ds(0, NK)] = high
+            r2[v, :, pl.ds(NK, NK)] = low
+        t = product(r2[...].reshape(FIELDS * CELLS, 2 * NK), w_k[...])
         for v in range(FIELDS):
-            change = dot(m_ij[...], t[v], ((1,), (0,)))
+            high, low = halves(t[v * CELLS : (v + 1) * CELLS])
+            w = jnp.concatenate([high, low], axis=1)
+            change = product(m2[...], jnp.concatenate([w, w], axis=0))
             if sweep == 0:
                 out[v] = change
                 inner = pl.ds(2 * NJ, CELLS)
@@ -288,26 +350,14 @@
         edge_i(sweep)
         for side in range(2):
             copies[sweep][0][side].start()
-        if sweep == 0:
-            for c in range(3):
-                n_k[c] = dot(pick, n[6 + c], ((1,), (1,)))
         edge_k(sweep)
         for side in range(2):
             copies[sweep][2][side].start()
         interior()
         if sweep == 0:
-            wide = lax.broadcasted_iota(jnp.int32, (CELLS, NI), 0)
-            e_i = jnp.where(
-                lax.shift_right_logical(wide, 3)
-                == lax.broadcasted_iota(jnp.int32, (CELLS, NI), 1), 1.0, 0.0,
-            ).astype(jnp.float32)
-            wide = lax.broadcasted_iota(jnp.int32, (CELLS, NJ), 0)
-            e_j = jnp.where(
-                jnp.bitwise_and(wide, 7) == lax.broadcasted_iota(jnp.int32, (CELLS, NJ), 1), 1.0, 0.0
-            ).astype(jnp.float32)
-            big_i = dot(dot(e_i, inv_i[...], ((1,), (0,))), e_i, ((1,), (1,)))
-            big_j = dot(dot(e_j, inv_j[...], ((1,), (0,))), e_j, ((1,), (1,)))
-            m_ij[...] = big_i * big_j
+            prepare()
+            load_rest[0].wait()
+            code, bit0, bit1, joined = read_codes()
         halo_k(sweep)
         halo_i(sweep)
         halo_j(sweep)
@@ -322,43 +372,54 @@
 def local(state, metrics, face_codes, inverse_i, inverse_j, inverse_k):
     f32 = jnp.float32
     vmem = pl.BlockSpec(memory_space=pltpu.VMEM)
-    anywhere = pl.BlockSpec(memory_space=pl.ANY)
+    hbm = pl.BlockSpec(memory_space=pltpu.HBM)
     result = pl.pallas_call(
         kernel,
         out_shape=jax.ShapeDtypeStruct((FIELDS, CELLS, NK), f32),
-        in_specs=[pl.BlockSpec(memory_space=pltpu.SMEM), anywhere, anywhere, vmem, vmem, vmem],
+        in_specs=[hbm] * 6,
         out_specs=vmem,
         scratch_shapes=[
+            pltpu.SMEM((1, 6), jnp.int32),
             pltpu.VMEM((FIELDS, CELLS + 4 * NJ, NK), f32),
             pltpu.VMEM((9, CELLS, NK), f32),
+            pltpu.VMEM((NI, NI), f32),
+            pltpu.VMEM((NJ, NJ), f32),
+            pltpu.VMEM((NK, NK), f32),
             pltpu.VMEM((FIELDS, CELLS, NK), f32),
             pltpu.VMEM((FIELDS, CELLS + 2 * NJ, NK), f32),
-            pltpu.VMEM((FIELDS, CELLS, NK), f32),
-            pltpu.VMEM((CELLS, CELLS), f32),
+            pltpu.VMEM((FIELDS, CELLS, 2 * NK), BF16),
+            pltpu.VMEM((2 * NK, 2 * NK), BF16),
+            pltpu.VMEM((CELLS, 2 * CELLS), BF16),
+            pltpu.VMEM((CELLS, NK), f32),
             pltpu.VMEM((3, 8, NK), f32),
             pltpu.VMEM((SWEEPS, 2, 2 * FIELDS, NJ, NK), f32),
             pltpu.VMEM((SWEEPS, 2, 2 * FIELDS, NI, NK), f32),
-            pltpu.VMEM((SWEEPS, 2, FIELDS, 8, NK), f32),
+            pltpu.VMEM((SWEEPS, FIELDS, 8, NK), f32),
             pltpu.VMEM((2, FIELDS, NJ, NK), f32),
             pltpu.VMEM((2, FIELDS, NI, NK), f32),
             pltpu.VMEM((FIELDS, 8, NK), f32),
             pltpu.VMEM((SWEEPS, 2, 2 * FIELDS, NJ, NK), f32),
             pltpu.VMEM((SWEEPS, 2, 2 * FIELDS, NI, NK), f32),
             pltpu.VMEM((SWEEPS, 2, FIELDS, 8, NK), f32),
-            pltpu.SemaphoreType.DMA((2,)),
+            pltpu.SemaphoreType.DMA((6,)),
             pltpu.SemaphoreType.DMA((SWEEPS, 3, 2)),
             pltpu.SemaphoreType.DMA((SWEEPS, 3, 2)),
         ],
-        compiler_params=pltpu.CompilerParams(collective_id=0, has_side_effects=True),
+        compiler_params=pltpu.CompilerParams(
+            collective_id=0, has_side_effects=True, vmem_limit_bytes=12 * 2**20
+        ),
         name="adi",
-    )(
-        face_codes.reshape(1, 6),
-        state.reshape(FIELDS, CELLS, NK),
-        metrics.reshape(9, CELLS, NK),
-        inverse_i.reshape(NI, NI),
-        inverse_j.reshape(NJ, NJ),
-        inverse_k.reshape(NK, NK),
-    )
+    )(*(
+        pltpu.with_memory_space_constraint(x, pltpu.HBM)
+        for x in (
+            face_codes.reshape(1, 6),
+            state.reshape(FIELDS, CELLS, NK),
+            metrics.reshape(9, CELLS, NK),
+            inverse_i.reshape(NI, NI),
+            inverse_j.reshape(NJ, NJ),
+            inverse_k.reshape(NK, NK),
+        )
+    ))
     return result.reshape(state.shape)
 
 

time: 30.3 us -> 25.6 us (0.84)
  the two profiles are of different devices: /device:TPU:16 before, /device:TPU:1 now
where the time goes in v2:
time: 25.6 us; the launch traced here: 25.4 us
  Pallas kernels  24.7 us (96%)
  local copies, waits for them, and re-layouts  0.73 us (3%)
    pallas_call x1, Pallas kernels, local(): pl.pallas_call(kernel, out_shape=jax.ShapeDtypeStruct((FIELDS, CELLS, NK)...  24.7 us
    unnamed x1, local copies, waits for them, and re-layouts  0.73 us

profile of v2, /device:TPU:1, one launch (start us, length us, event | category | flops | bytes accessed | tf_op | source)
XLA Modules:
  0.0 25.4 jit_solution(8382823190825804013)
XLA Ops:
  0.0 24.7 %adi.1 = f32[5,128,128]{2,1,0:T(8,128)S(1)} custom-call(s32[1,6]{1,0:T(1,128)} %bitcast.13, f32[5,128,128]{2,1,0:T(8,128)} %bitcast.9, f32[9,128,128]{2,1,0:T(8,128)} %bitcast.8, f32[16,16]{1,0:T(8,128)} %bitcast.11, f32[8,8]{1,0:T(8,128)} %bitcast.12, f32[128,128]{1,0:T(8,128)} %bitcast.10), custom_call_target="tpu_custom_call" | custom-call | tf_op jit(solution)/shard_map/adi/pallas_call | solution.py:376
  24.7 0.7 %copy.8 = f32[5,16,8,128]{3,2,1,0:T(8,128)} copy(f32[5,16,8,128]{3,2,1,0:T(8,128)S(1)} %bitcast.7) | data formatting | bytes 655360

commit v3 on v2

--- a/solution.py
+++ b/solution.py
@@ -15,6 +15,7 @@
 FIELDS = 5
 NI, NJ, NK = 16, 8, 128
 CELLS = NI * NJ
+LATE = 4 * NJ + 2 * NI
 
 gas_factor = 0.4
 damping = 0.1
@@ -63,10 +64,7 @@
 
 
 def product(a, b):
-    both = lax.dot_general(
-        a, b, (((1,), (0,)), ((), ())), preferred_element_type=jnp.float32
-    )
-    return both[:, :NK] + both[:, NK:]
+    return lax.dot_general(a, b, (((1,), (0,)), ((), ())), preferred_element_type=jnp.float32)
 
 
 def lanes(x, index):
@@ -79,7 +77,7 @@
 
 def kernel(
     codes_hbm, state, metrics, inv_i_hbm, inv_j_hbm, inv_k_hbm, out,
-    codes, u, n, inv_i, inv_j, inv_k, r, gi, r2, w_k, m2, cross, n_k,
+    codes, u, n, inv_i, inv_j, inv_k, r, late, gi, w_k, m3, late3, cross, n_k,
     send_i, send_j, send_k, keep_i, keep_j, keep_k, recv_i, recv_j, recv_k,
     load_sem, send_sem, recv_sem,
 ):
@@ -96,19 +94,22 @@
     for load in load_rest:
         load.start()
 
-    near = []
-    for axis in AXES:
-        size, me = lax.axis_size(axis), lax.axis_index(axis)
-        near.append((lax.rem(me + size - 1, size), lax.rem(me + 1, size)))
+    size = [lax.axis_size(axis) for axis in AXES]
+    me = [lax.axis_index(axis) for axis in AXES]
+
+    def neighbour(d, side):
+        return lax.rem(me[d] + size[d] - 1 + 2 * side, size[d])
+
     barrier = pltpu.get_barrier_semaphore()
     for d, axis in enumerate(AXES):
         for side in range(2):
             pl.semaphore_signal(
-                barrier, inc=1, device_id={axis: near[d][side]}, device_id_type=MESH
+                barrier, inc=1, device_id={axis: neighbour(d, side)}, device_id_type=MESH
             )
 
     sends = (send_i, send_j, send_k)
     recvs = (recv_i, recv_j, recv_k)
+    far_side = [lax.rem(me[d], 2) for d in range(2)]
 
     def copy(sweep, d, side):
         return pltpu.make_async_remote_copy(
@@ -116,11 +117,9 @@
             dst_ref=recvs[d].at[sweep, 1 - side],
             send_sem=send_sem.at[sweep, d, side],
             recv_sem=recv_sem.at[sweep, d, 1 - side],
-            device_id={AXES[d]: near[d][side]},
+            device_id={AXES[d]: neighbour(d, side)},
             device_id_type=MESH,
         )
-
-    copies = [[[copy(s, d, side) for side in range(2)] for d in range(3)] for s in range(SWEEPS)]
 
     sub = lax.broadcasted_iota(jnp.int32, (8, NK), 0)
     lane = lax.broadcasted_iota(jnp.int32, (8, NK), 1)
@@ -132,13 +131,6 @@
     last_k4 = jnp.logical_or(lane < 2, lane >= NK - 2)
     lane_rev_i = jnp.bitwise_xor(lane, CELLS - NJ)
     lane_rev_j = jnp.bitwise_xor(lane, NJ - 1)
-
-    def read_codes():
-        code = [jnp.full((8, NK), codes[0, q], jnp.int32) for q in range(6)]
-        bit0 = [jnp.bitwise_and(c - 1, 1) == 1 for c in code]
-        bit1 = [jnp.bitwise_and(c - 1, 2) == 2 for c in code]
-        joined = [c > 0 for c in code]
-        return code, bit0, bit1, joined
 
     zero = jnp.zeros((2 * NJ, NK), jnp.float32)
     for v in range(FIELDS):
@@ -231,7 +223,7 @@
                 r[v, pl.ds(at, NJ), :] = total[v]
             return carry
 
-        lax.fori_loop(0, NI, slab, 0)
+        lax.fori_loop(0, NI, slab, 0, unroll=4)
 
         def chord(i, carry):
             at = pl.multiple_of(i * NJ, NJ)
@@ -246,14 +238,15 @@
                 )
             return carry
 
-        lax.fori_loop(0, NI, chord, 0)
+        lax.fori_loop(0, NI, chord, 0, unroll=4)
 
     def halo_k(sweep):
         for side in range(2):
-            copies[sweep][2][1 - side].wait_recv()
-        flip_i = jnp.bitwise_and(jnp.where(top_k, code[5], code[4]) - 1, 1) == 1
-        flip_j = jnp.bitwise_and(jnp.where(top_k, code[5], code[4]) - 1, 2) == 2
-        linked = jnp.where(top_k, code[5], code[4]) > 0
+            copy(sweep, 2, side).wait_recv()
+        code = [jnp.full((8, NK), codes[0, q], jnp.int32) for q in range(4, 6)]
+        flip_i = jnp.bitwise_and(jnp.where(top_k, code[1], code[0]) - 1, 1) == 1
+        flip_j = jnp.bitwise_and(jnp.where(top_k, code[1], code[0]) - 1, 2) == 2
+        linked = jnp.where(top_k, code[1], code[0]) > 0
         for v in range(FIELDS):
             z = jnp.where(top_k, recv_k[sweep, 1, v], recv_k[sweep, 0, v])
             z = jnp.where(flip_i, lanes(z, lane_rev_i), z)
@@ -268,37 +261,44 @@
                     last_k4, pltpu.roll(x, NK - 2 - 8 * v, 1), 0.0
                 )
 
-    def halo_i(sweep):
-        for side in range(2):
-            copies[sweep][0][1 - side].wait_recv()
-            face = side
-            for q in range(2 * FIELDS):
-                v = q % FIELDS
-                x = recv_i[sweep, side, q]
-                x = jnp.where(bit0[face], rows(x, row_rev), x)
-                x = jnp.where(bit1[face], lanes(x, lane_rev), x)
-                own = keep_i[side, v] if q < FIELDS else send_i[sweep, side, q]
-                x = jnp.where(joined[face], x, own)
-                depth = 0 if q < FIELDS else 1
-                at = (depth if side == 0 else NI - 1 - depth) * NJ
-                r[v, pl.ds(at, NJ), :] = r[v, pl.ds(at, NJ), :] + x
-
-    def halo_j(sweep):
-        for side in range(2):
-            copies[sweep][1][1 - side].wait_recv()
-            face = 2 + side
-            for q in range(2 * FIELDS):
-                v = q % FIELDS
-                x = [recv_j[sweep, side, q, pl.ds(8 * h, 8), :] for h in range(2)]
-                rev = [rows(x[1 - h], row_rev) for h in range(2)]
-                x = [jnp.where(bit0[face], rev[h], x[h]) for h in range(2)]
-                x = [jnp.where(bit1[face], lanes(x[h], lane_rev), x[h]) for h in range(2)]
-                depth = 0 if q < FIELDS else 1
-                at = depth if side == 0 else NJ - 1 - depth
-                for h in range(2):
-                    part = pl.ds(8 * h, 8)
-                    own = keep_j[side, v, part, :] if q < FIELDS else send_j[sweep, side, q, part, :]
-                    y = jnp.where(joined[face], x[h], own)
+    def orientation(d, side):
+        code = jnp.full((8, NK), codes[0, 2 * d + side], jnp.int32)
+        first = jnp.bitwise_and(code - 1, 1) == 1
+        second = jnp.bitwise_and(code - 1, 2) == 2
+        return first, second, code > 0
+
+    def halo_i(sweep, side):
+        copy(sweep, 0, 1 - side).wait_recv()
+        first, second, linked = orientation(0, side)
+        for q in range(2 * FIELDS):
+            v = q % FIELDS
+            x = recv_i[sweep, side, q]
+            x = jnp.where(first, rows(x, row_rev), x)
+            x = jnp.where(second, lanes(x, lane_rev), x)
+            own = keep_i[side, v] if q < FIELDS else send_i[sweep, side, q]
+            x = jnp.where(linked, x, own)
+            depth = 0 if q < FIELDS else 1
+            at = pl.multiple_of((2 * side + depth) * NJ, NJ)
+            late[v, pl.ds(at, NJ), :] = x
+
+    def halo_j(sweep, side, far):
+        copy(sweep, 1, 1 - side).wait_recv()
+        first, second, linked = orientation(1, side)
+        for q in range(2 * FIELDS):
+            v = q % FIELDS
+            x = [recv_j[sweep, side, q, pl.ds(8 * h, 8), :] for h in range(2)]
+            rev = [rows(x[1 - h], row_rev) for h in range(2)]
+            x = [jnp.where(first, rev[h], x[h]) for h in range(2)]
+            x = [jnp.where(second, lanes(x[h], lane_rev), x[h]) for h in range(2)]
+            depth = 0 if q < FIELDS else 1
+            at = side * (NJ - 1) + (1 - 2 * side) * depth
+            for h in range(2):
+                part = pl.ds(8 * h, 8)
+                own = keep_j[side, v, part, :] if q < FIELDS else send_j[sweep, side, q, part, :]
+                y = jnp.where(linked, x[h], own)
+                if far:
+                    late[v, pl.ds(4 * NJ + depth * NI + 8 * h, 8), :] = y
+                else:
                     where = pl.ds(8 * h * NJ + at, 8, stride=NJ)
                     r[v, where, :] = r[v, where, :] + y
 
@@ -306,67 +306,103 @@
         for load in load_rest[1:]:
             load.wait()
         high, low = halves(jnp.transpose(inv_k[...]))
-        for h in range(2):
-            w_k[pl.ds(h * NK, NK), pl.ds(0, NK)] = high
-            w_k[pl.ds(h * NK, NK), pl.ds(NK, NK)] = low
-        wide = lax.broadcasted_iota(jnp.int32, (CELLS, NI), 0)
-        e_i = jnp.where(
-            lax.shift_right_logical(wide, 3)
-            == lax.broadcasted_iota(jnp.int32, (CELLS, NI), 1), 1.0, 0.0,
-        ).astype(jnp.float32)
-        wide = lax.broadcasted_iota(jnp.int32, (CELLS, NJ), 0)
-        e_j = jnp.where(
-            jnp.bitwise_and(wide, 7) == lax.broadcasted_iota(jnp.int32, (CELLS, NJ), 1), 1.0, 0.0
-        ).astype(jnp.float32)
-        big_i = dot(dot(e_i, inv_i[...], ((1,), (0,))), e_i, ((1,), (1,)))
-        big_j = dot(dot(e_j, inv_j[...], ((1,), (0,))), e_j, ((1,), (1,)))
-        high, low = halves(big_i * big_j)
-        m2[:, pl.ds(0, CELLS)] = high
-        m2[:, pl.ds(CELLS, CELLS)] = low
+        for h, part in enumerate((high, high, low)):
+            w_k[pl.ds(h * NK, NK), :] = part
+        def one_hot(index, shape):
+            return jnp.where(index == lax.broadcasted_iota(jnp.int32, shape, 1), 1.0, 0.0).astype(
+                jnp.float32
+            )
+
+        def taken(one, x):
+            high, low = halves(x)
+            return product(
+                jnp.concatenate([one, one], axis=1).astype(BF16), jnp.concatenate([high, low], axis=0)
+            )
+
+        def pair(block_i, block_j):
+            return taken(all_i, jnp.transpose(taken(block_i, t_i))) * taken(
+                all_j, jnp.transpose(taken(block_j, t_j))
+            )
+
+        cell = lax.broadcasted_iota(jnp.int32, (CELLS, NI), 0)
+        all_i = one_hot(lax.shift_right_logical(cell, 3), (CELLS, NI))
+        cell = lax.broadcasted_iota(jnp.int32, (CELLS, NJ), 0)
+        all_j = one_hot(jnp.bitwise_and(cell, 7), (CELLS, NJ))
+        t_i = jnp.transpose(inv_i[...])
+        t_j = jnp.transpose(inv_j[...])
+        q = lax.broadcasted_iota(jnp.int32, (LATE, NI), 0)
+        layer = lax.shift_right_logical(q, 3)
+        edge = jnp.where(layer < 2, layer, NI + 1 - layer)
+        late_i = one_hot(jnp.where(q < 4 * NJ, edge, jnp.bitwise_and(q, NI - 1)), (LATE, NI))
+        q = lax.broadcasted_iota(jnp.int32, (LATE, NJ), 0)
+        depth = jnp.where(q < 4 * NJ + NI, 0, 1)
+        edge = far_side[1] * (NJ - 1) + (1 - 2 * far_side[1]) * depth
+        late_j = one_hot(jnp.where(q < 4 * NJ, jnp.bitwise_and(q, 7), edge), (LATE, NJ))
+        high, low = halves(pair(all_i, all_j))
+        for h, part in enumerate((high, low, high)):
+            m3[:, pl.ds(h * CELLS, CELLS)] = part
+        high, low = halves(pair(late_i, late_j))
+        late3[...] = jnp.concatenate([high, low, high], axis=1)
+
+    def add(sweep, v, change, first):
+        if sweep == 0 and first:
+            out[v] = change
+        else:
+            out[v] = out[v] + change
+        if sweep == 0:
+            inner = pl.ds(2 * NJ, CELLS)
+            u[v, inner, :] = u[v, inner, :] + pseudo_step * change
+
+    def solve_late(sweep):
+        high, low = halves(late[...].reshape(FIELDS * LATE, NK))
+        t = product(jnp.concatenate([high, low, high], axis=1), w_k[...])
+        for group in ((0, 1, 2, 3), (4,)):
+            high, low = halves(
+                jnp.concatenate([t[v * LATE : (v + 1) * LATE] for v in group], axis=1)
+            )
+            both = product(late3[...], jnp.concatenate([high, high, low], axis=0))
+            for q, v in enumerate(group):
+                add(sweep, v, both[:, q * NK : (q + 1) * NK], False)
 
     def solve(sweep):
-        for v in range(FIELDS):
-            high, low = halves(r[v])
-            r2[v, :, pl.ds(0, NK)] = high
-            r2[v, :, pl.ds(NK, NK)] = low
-        t = product(r2[...].reshape(FIELDS * CELLS, 2 * NK), w_k[...])
-        for v in range(FIELDS):
-            high, low = halves(t[v * CELLS : (v + 1) * CELLS])
-            w = jnp.concatenate([high, low], axis=1)
-            change = product(m2[...], jnp.concatenate([w, w], axis=0))
-            if sweep == 0:
-                out[v] = change
-                inner = pl.ds(2 * NJ, CELLS)
-                u[v, inner, :] = u[v, inner, :] + pseudo_step * change
-            else:
-                out[v] = out[v] + change
+        for group in ((0, 1), (2, 3), (4,)):
+            high, low = halves(jnp.concatenate([r[v] for v in group], axis=0))
+            t = product(jnp.concatenate([high, low, high], axis=1), w_k[...])
+            high, low = halves(
+                jnp.concatenate([t[q * CELLS : (q + 1) * CELLS] for q in range(len(group))], axis=1)
+            )
+            both = product(m3[...], jnp.concatenate([high, high, low], axis=0))
+            for q, v in enumerate(group):
+                add(sweep, v, both[:, q * NK : (q + 1) * NK], True)
 
     for sweep in range(SWEEPS):
-        edge_j(sweep)
+        edge_i(sweep)
         if sweep == 0:
             pl.semaphore_wait(barrier, 6)
-        for side in range(2):
-            copies[sweep][1][side].start()
-        edge_i(sweep)
-        for side in range(2):
-            copies[sweep][0][side].start()
+        edge_j(sweep)
+        copy(sweep, 1, far_side[1]).start()
+        copy(sweep, 0, far_side[0]).start()
         edge_k(sweep)
         for side in range(2):
-            copies[sweep][2][side].start()
+            copy(sweep, 2, side).start()
+        copy(sweep, 0, 1 - far_side[0]).start()
+        copy(sweep, 1, 1 - far_side[1]).start()
         interior()
         if sweep == 0:
             prepare()
             load_rest[0].wait()
-            code, bit0, bit1, joined = read_codes()
+        halo_j(sweep, 1 - far_side[1], False)
         halo_k(sweep)
-        halo_i(sweep)
-        halo_j(sweep)
         solve(sweep)
+        halo_i(sweep, 1 - far_side[0])
+        halo_j(sweep, far_side[1], True)
+        halo_i(sweep, far_side[0])
+        solve_late(sweep)
 
     for sweep in range(SWEEPS):
         for d in range(3):
             for side in range(2):
-                copies[sweep][d][side].wait_send()
+                copy(sweep, d, side).wait_send()
 
 
 def local(state, metrics, face_codes, inverse_i, inverse_j, inverse_k):
@@ -386,10 +422,11 @@
             pltpu.VMEM((NJ, NJ), f32),
             pltpu.VMEM((NK, NK), f32),
             pltpu.VMEM((FIELDS, CELLS, NK), f32),
+            pltpu.VMEM((FIELDS, LATE, NK), f32),
             pltpu.VMEM((FIELDS, CELLS + 2 * NJ, NK), f32),
-            pltpu.VMEM((FIELDS, CELLS, 2 * NK), BF16),
-            pltpu.VMEM((2 * NK, 2 * NK), BF16),
-            pltpu.VMEM((CELLS, 2 * CELLS), BF16),
+            pltpu.VMEM((3 * NK, NK), BF16),
+            pltpu.VMEM((CELLS, 3 * CELLS), BF16),
+            pltpu.VMEM((CELLS, 3 * LATE), BF16),
             pltpu.VMEM((CELLS, NK), f32),
             pltpu.VMEM((3, 8, NK), f32),
             pltpu.VMEM((SWEEPS, 2, 2 * FIELDS, NJ, NK), f32),

time: 25.6 us -> 24.9 us (0.973)
  Pallas kernels: 24.7 us -> 23.9 us
    pallas_call x1, Pallas kernels: 24.7 us -> 23.9 us  [local(): pl.pallas_call(kernel, out_shape=jax.ShapeDtypeStruct((FIELDS, CELLS, NK)...]
where the time goes in v3:
time: 24.9 us; the launch traced here: 24.6 us
  Pallas kernels  23.9 us (96%)
  local copies, waits for them, and re-layouts  0.73 us (3%)
    pallas_call x1, Pallas kernels, local(): pl.pallas_call(kernel, out_shape=jax.ShapeDtypeStruct((FIELDS, CELLS, NK)...  23.9 us
    unnamed x1, local copies, waits for them, and re-layouts  0.73 us

profile of v3, /device:TPU:1, one launch (start us, length us, event | category | flops | bytes accessed | tf_op | source)
XLA Modules:
  0.0 24.6 jit_solution(1368251969103487379)
XLA Ops:
  0.0 23.9 %adi.1 = f32[5,128,128]{2,1,0:T(8,128)S(1)} custom-call(s32[1,6]{1,0:T(1,128)} %bitcast.13, f32[5,128,128]{2,1,0:T(8,128)} %bitcast.9, f32[9,128,128]{2,1,0:T(8,128)} %bitcast.8, f32[16,16]{1,0:T(8,128)} %bitcast.11, f32[8,8]{1,0:T(8,128)} %bitcast.12, f32[128,128]{1,0:T(8,128)} %bitcast.10), custom_call_target="tpu_custom_call" | custom-call | tf_op jit(solution)/shard_map/adi/pallas_call | solution.py:412
  23.9 0.7 %copy.8 = f32[5,16,8,128]{3,2,1,0:T(8,128)} copy(f32[5,16,8,128]{3,2,1,0:T(8,128)S(1)} %bitcast.7) | data formatting | bytes 655360

commit v4 on v3

--- a/solution.py
+++ b/solution.py
@@ -89,10 +89,10 @@
             (codes_hbm, codes), (inv_i_hbm, inv_i), (inv_j_hbm, inv_j), (inv_k_hbm, inv_k),
         ))
     ]
+    for load in load_rest[::-1]:
+        load.start()
     load_u.start()
     load_n.start()
-    for load in load_rest:
-        load.start()
 
     size = [lax.axis_size(axis) for axis in AXES]
     me = [lax.axis_index(axis) for axis in AXES]
@@ -140,6 +140,50 @@
         gi[v, pl.ds(NJ + CELLS, NJ), :] = zero[:NJ]
     cross[...] = jnp.zeros((CELLS, NK), jnp.float32)
 
+    def prepare():
+        for load in load_rest[1:]:
+            load.wait()
+        high, low = halves(jnp.transpose(inv_k[...]))
+        for h, part in enumerate((high, high, low)):
+            w_k[pl.ds(h * NK, NK), :] = part
+        def one_hot(index, shape):
+            return jnp.where(index == lax.broadcasted_iota(jnp.int32, shape, 1), 1.0, 0.0).astype(
+                jnp.float32
+            )
+
+        def taken(one, x):
+            high, low = halves(x)
+            return product(
+                jnp.concatenate([one, one], axis=1).astype(BF16), jnp.concatenate([high, low], axis=0)
+            )
+
+        def pair(block_i, block_j):
+            return taken(all_i, jnp.transpose(taken(block_i, t_i))) * taken(
+                all_j, jnp.transpose(taken(block_j, t_j))
+            )
+
+        cell = lax.broadcasted_iota(jnp.int32, (CELLS, NI), 0)
+        all_i = one_hot(lax.shift_right_logical(cell, 3), (CELLS, NI))
+        cell = lax.broadcasted_iota(jnp.int32, (CELLS, NJ), 0)
+        all_j = one_hot(jnp.bitwise_and(cell, 7), (CELLS, NJ))
+        t_i = jnp.transpose(inv_i[...])
+        t_j = jnp.transpose(inv_j[...])
+        q = lax.broadcasted_iota(jnp.int32, (LATE, NI), 0)
+        layer = lax.shift_right_logical(q, 3)
+        edge = jnp.where(layer < 2, layer, NI + 1 - layer)
+        late_i = one_hot(jnp.where(q < 4 * NJ, edge, jnp.bitwise_and(q, NI - 1)), (LATE, NI))
+        q = lax.broadcasted_iota(jnp.int32, (LATE, NJ), 0)
+        depth = jnp.where(q < 4 * NJ + NI, 0, 1)
+        edge = far_side[1] * (NJ - 1) + (1 - 2 * far_side[1]) * depth
+        late_j = one_hot(jnp.where(q < 4 * NJ, jnp.bitwise_and(q, 7), edge), (LATE, NJ))
+        high, low = halves(pair(all_i, all_j))
+        for h, part in enumerate((high, low, high)):
+            m3[:, pl.ds(h * CELLS, CELLS)] = part
+        high, low = halves(pair(late_i, late_j))
+        late3[...] = jnp.concatenate([high, low, high], axis=1)
+
+    prepare()
+    load_rest[0].wait()
     load_u.wait()
     load_n.wait()
 
@@ -268,7 +312,6 @@
         return first, second, code > 0
 
     def halo_i(sweep, side):
-        copy(sweep, 0, 1 - side).wait_recv()
         first, second, linked = orientation(0, side)
         for q in range(2 * FIELDS):
             v = q % FIELDS
@@ -282,7 +325,8 @@
             late[v, pl.ds(at, NJ), :] = x
 
     def halo_j(sweep, side, far):
-        copy(sweep, 1, 1 - side).wait_recv()
+        if not far:
+            copy(sweep, 1, 1 - side).wait_recv()
         first, second, linked = orientation(1, side)
         for q in range(2 * FIELDS):
             v = q % FIELDS
@@ -302,48 +346,6 @@
                     where = pl.ds(8 * h * NJ + at, 8, stride=NJ)
                     r[v, where, :] = r[v, where, :] + y
 
-    def prepare():
-        for load in load_rest[1:]:
-            load.wait()
-        high, low = halves(jnp.transpose(inv_k[...]))
-        for h, part in enumerate((high, high, low)):
-            w_k[pl.ds(h * NK, NK), :] = part
-        def one_hot(index, shape):
-            return jnp.where(index == lax.broadcasted_iota(jnp.int32, shape, 1), 1.0, 0.0).astype(
-                jnp.float32
-            )
-
-        def taken(one, x):
-            high, low = halves(x)
-            return product(
-                jnp.concatenate([one, one], axis=1).astype(BF16), jnp.concatenate([high, low], axis=0)
-            )
-
-        def pair(block_i, block_j):
-            return taken(all_i, jnp.transpose(taken(block_i, t_i))) * taken(
-                all_j, jnp.transpose(taken(block_j, t_j))
-            )
-
-        cell = lax.broadcasted_iota(jnp.int32, (CELLS, NI), 0)
-        all_i = one_hot(lax.shift_right_logical(cell, 3), (CELLS, NI))
-        cell = lax.broadcasted_iota(jnp.int32, (CELLS, NJ), 0)
-        all_j = one_hot(jnp.bitwise_and(cell, 7), (CELLS, NJ))
-        t_i = jnp.transpose(inv_i[...])
-        t_j = jnp.transpose(inv_j[...])
-        q = lax.broadcasted_iota(jnp.int32, (LATE, NI), 0)
-        layer = lax.shift_right_logical(q, 3)
-        edge = jnp.where(layer < 2, layer, NI + 1 - layer)
-        late_i = one_hot(jnp.where(q < 4 * NJ, edge, jnp.bitwise_and(q, NI - 1)), (LATE, NI))
-        q = lax.broadcasted_iota(jnp.int32, (LATE, NJ), 0)
-        depth = jnp.where(q < 4 * NJ + NI, 0, 1)
-        edge = far_side[1] * (NJ - 1) + (1 - 2 * far_side[1]) * depth
-        late_j = one_hot(jnp.where(q < 4 * NJ, jnp.bitwise_and(q, 7), edge), (LATE, NJ))
-        high, low = halves(pair(all_i, all_j))
-        for h, part in enumerate((high, low, high)):
-            m3[:, pl.ds(h * CELLS, CELLS)] = part
-        high, low = halves(pair(late_i, late_j))
-        late3[...] = jnp.concatenate([high, low, high], axis=1)
-
     def add(sweep, v, change, first):
         if sweep == 0 and first:
             out[v] = change
@@ -388,12 +390,12 @@
         copy(sweep, 0, 1 - far_side[0]).start()
         copy(sweep, 1, 1 - far_side[1]).start()
         interior()
-        if sweep == 0:
-            prepare()
-            load_rest[0].wait()
         halo_j(sweep, 1 - far_side[1], False)
         halo_k(sweep)
         solve(sweep)
+        copy(sweep, 0, 0).wait_recv()
+        copy(sweep, 0, 1).wait_recv()
+        copy(sweep, 1, 1 - far_side[1]).wait_recv()
         halo_i(sweep, 1 - far_side[0])
         halo_j(sweep, far_side[1], True)
         halo_i(sweep, far_side[0])

time: 24.9 us -> 24.8 us (level)
    pallas_call x1, Pallas kernels: 23.9 us -> 23.7 us  [local(): pl.pallas_call(kernel, out_shape=jax.ShapeDtypeStruct((FIELDS, CELLS, NK)...]
where the time goes in v4:
time: 24.8 us; the launch traced here: 24.4 us
  Pallas kernels  23.7 us (96%)
  local copies, waits for them, and re-layouts  0.73 us (3%)
    pallas_call x1, Pallas kernels, local(): pl.pallas_call(kernel, out_shape=jax.ShapeDtypeStruct((FIELDS, CELLS, NK)...  23.7 us
    unnamed x1, local copies, waits for them, and re-layouts  0.73 us

profile of v4, /device:TPU:1, one launch (start us, length us, event | category | flops | bytes accessed | tf_op | source)
XLA Modules:
  0.0 24.4 jit_solution(367304610015348797)
XLA Ops:
  0.0 23.7 %adi.1 = f32[5,128,128]{2,1,0:T(8,128)S(1)} custom-call(s32[1,6]{1,0:T(1,128)} %bitcast.13, f32[5,128,128]{2,1,0:T(8,128)} %bitcast.9, f32[9,128,128]{2,1,0:T(8,128)} %bitcast.8, f32[16,16]{1,0:T(8,128)} %bitcast.11, f32[8,8]{1,0:T(8,128)} %bitcast.12, f32[128,128]{1,0:T(8,128)} %bitcast.10), custom_call_target="tpu_custom_call" | custom-call | tf_op jit(solution)/shard_map/adi/pallas_call | solution.py:414
  23.7 0.7 %copy.8 = f32[5,16,8,128]{3,2,1,0:T(8,128)} copy(f32[5,16,8,128]{3,2,1,0:T(8,128)S(1)} %bitcast.7) | data formatting | bytes 655360

commit v5 on v4

--- a/solution.py
+++ b/solution.py
@@ -89,10 +89,6 @@
             (codes_hbm, codes), (inv_i_hbm, inv_i), (inv_j_hbm, inv_j), (inv_k_hbm, inv_k),
         ))
     ]
-    for load in load_rest[::-1]:
-        load.start()
-    load_u.start()
-    load_n.start()
 
     size = [lax.axis_size(axis) for axis in AXES]
     me = [lax.axis_index(axis) for axis in AXES]
@@ -107,6 +103,10 @@
                 barrier, inc=1, device_id={axis: neighbour(d, side)}, device_id_type=MESH
             )
 
+    for load in load_rest[::-1]:
+        load.start()
+    load_u.start()
+    load_n.start()
     sends = (send_i, send_j, send_k)
     recvs = (recv_i, recv_j, recv_k)
     far_side = [lax.rem(me[d], 2) for d in range(2)]

time: 24.8 us -> 24.8 us (level)
  no operation moved by 1% of the time
where the time goes in v5:
time: 24.8 us; the launch traced here: 24.4 us
  Pallas kernels  23.6 us (95%)
  local copies, waits for them, and re-layouts  0.73 us (3%)
    pallas_call x1, Pallas kernels, local(): pl.pallas_call(kernel, out_shape=jax.ShapeDtypeStruct((FIELDS, CELLS, NK)...  23.6 us
    unnamed x1, local copies, waits for them, and re-layouts  0.73 us

profile of v5, /device:TPU:1, one launch (start us, length us, event | category | flops | bytes accessed | tf_op | source)
XLA Modules:
  0.0 24.4 jit_solution(16134521955393291010)
XLA Ops:
  0.0 23.6 %adi.1 = f32[5,128,128]{2,1,0:T(8,128)S(1)} custom-call(s32[1,6]{1,0:T(1,128)} %bitcast.13, f32[5,128,128]{2,1,0:T(8,128)} %bitcast.9, f32[9,128,128]{2,1,0:T(8,128)} %bitcast.8, f32[16,16]{1,0:T(8,128)} %bitcast.11, f32[8,8]{1,0:T(8,128)} %bitcast.12, f32[128,128]{1,0:T(8,128)} %bitcast.10), custom_call_target="tpu_custom_call" | custom-call | tf_op jit(solution)/shard_map/adi/pallas_call | solution.py:414
  23.7 0.7 %copy.8 = f32[5,16,8,128]{3,2,1,0:T(8,128)} copy(f32[5,16,8,128]{3,2,1,0:T(8,128)S(1)} %bitcast.7) | data formatting | bytes 655360
